TPU v7x, 128 devices: a whole 4x4x4 slice. The times are simulated.
128 devices in a mesh: panel: 32 (over z, x, core), slab: 4 (over y).
Axes of the slice: x: 4, y: 4, z: 4, core: 2. Of those that a mesh axis runs over, the one named last changes fastest.
Arguments:
- charges: bfloat16 [1048576], P(('panel', 'slab')), may hold values from -6 to 6
- target: float32 [1048576], P(('panel', 'slab')), may hold values from -6 to 6
- stencil: bfloat16 [16384, 64, 256], P(('panel', 'slab')), may hold values from -0.375 to 0.375
- near_matrix: bfloat16 [16384, 4, 4096], P(('panel', 'slab')), may hold values from -0.375 to 0.375
- green: float32 [4096, 4096], P(None, ('panel', 'slab')), may hold values from 0.5 to 8
- block_dest: int32 [16384, 1], P(('panel', 'slab')), may hold values from 0 to 127; in each aligned block of 128 rows (0 to 127, 128 to 255, ...) at most 2 rows name the same one
- block_tile: int32 [16384], P(('panel', 'slab')), may hold values from 0 to 511
- near_offset: int32 [16384, 4], P(('panel', 'slab')), may hold values from -8 to 8
Outputs:
- potentials: float32 [1048576], P(('panel', 'slab'))
- gradient: float32 [1048576], P(('panel', 'slab'))
Inputs may be any that keep to these rules, and one draw needn't show every extreme that they name: `block_dest`: in the 128 blocks of one device no owner is named more than 2 times; in some device's blocks one owner is named exactly 2 times.
All inputs are finite; a program needn't handle non-finite values.
Results may differ from a plain program's by a relative error of at most 0.0025.
The roundings to bfloat16 on the way count: a program that leaves them out, or rounds other values in their place, can miss the bound.
Values may be sent and summed in bfloat16 or wider, within the bound.
A program may use at most 128 MiB of HBM per device.

v0:
```python
import math

import jax
import jax.numpy as jnp
from jax import lax
from jax.sharding import PartitionSpec as P

GRID = 4096
TILE = 16
REACH = 8


HIGHEST = lax.Precision.HIGHEST


def extended_2(cells, sides, width):
    for axis, dim in sides:
        count = lax.axis_size(axis)
        ends = count - 1
        head = lax.slice_in_dim(cells, 0, width, axis=dim)
        tail = lax.slice_in_dim(cells, cells.shape[dim] - width, cells.shape[dim], axis=dim)
        cells = jnp.concatenate(
            [
                lax.ppermute(tail, axis, [(i, (i + 1) % count) for i in range(ends)]),
                cells,
                lax.ppermute(head, axis, [((i + 1) % count, i) for i in range(ends)]),
            ],
            axis=dim,
        )
    return cells


def tables(size_in, size_out, modulus, direction):
    row_index = lax.broadcasted_iota(jnp.int32, (size_in, size_out), 0)
    col_index = lax.broadcasted_iota(jnp.int32, (size_in, size_out), 1)
    phase_angle = (
        direction * 2.0 * math.pi / modulus * (row_index * col_index % modulus).astype(jnp.float32)
    )
    return (jnp.cos(phase_angle), jnp.sin(phase_angle))


def rotate(stacked, formula, cosine, sine):
    with_cos = jnp.einsum(formula, stacked, cosine, precision=HIGHEST)
    with_sin = jnp.einsum(formula, stacked, sine, precision=HIGHEST)
    return jnp.stack([with_cos[0] - with_sin[1], with_sin[0] + with_cos[1]])


def twiddle(stacked, cosine, sine):
    return jnp.stack(
        [stacked[0] * cosine - stacked[1] * sine, stacked[0] * sine + stacked[1] * cosine]
    )


def convolve(grid_cells, green_local, devices, regroup):
    row_count = grid_cells.shape[0]
    width = GRID // devices
    shaped = grid_cells.reshape(row_count, width, devices)
    inner_cos, inner_sin = tables(width, width, width, -1.0)
    outer_cos, outer_sin = tables(devices, devices, devices, -1.0)
    local_cos, local_sin = tables(row_count, row_count, row_count, -1.0)
    twist_cos, twist_sin = tables(width, devices, GRID, -1.0)
    spin_cos, spin_sin = tables(row_count, devices, GRID, -1.0)
    partial_value = jnp.stack(
        [
            jnp.einsum("rab,ak->rkb", shaped, inner_cos, precision=HIGHEST),
            jnp.einsum("rab,ak->rkb", shaped, inner_sin, precision=HIGHEST),
        ]
    )
    partial_value = twiddle(partial_value, twist_cos[None], twist_sin[None])
    spectrum = rotate(partial_value, "zrab,bk->zrka", outer_cos, outer_sin)
    spectrum = regroup(spectrum)
    spectrum = rotate(spectrum, "zrsc,sk->zrkc", outer_cos, outer_sin)
    spectrum = twiddle(spectrum, spin_cos[:, :, None], spin_sin[:, :, None])
    spectrum = rotate(spectrum, "zrkc,rm->zmkc", local_cos, local_sin)
    spectrum = spectrum * green_local.reshape(row_count, devices, width)[None]
    spectrum = rotate(spectrum, "zmkc,mq->zqkc", local_cos, -local_sin)
    spectrum = twiddle(spectrum, spin_cos[:, :, None], -spin_sin[:, :, None])
    spectrum = rotate(spectrum, "zqkc,ks->zqsc", outer_cos, -outer_sin)
    spectrum = regroup(spectrum)
    spectrum = rotate(spectrum, "zrka,kq->zrqa", outer_cos, -outer_sin)
    spectrum = twiddle(spectrum, twist_cos.T[None], -twist_sin.T[None])
    real_out = jnp.einsum("rqk,kp->rpq", spectrum[0], inner_cos, precision=HIGHEST)
    real_out = real_out + jnp.einsum("rqk,kp->rpq", spectrum[1], inner_sin, precision=HIGHEST)
    return real_out.reshape(row_count, GRID) * (1.0 / (GRID * GRID))


def local(charges, target, stencil, near_matrix, green, block_dest, block_tile, near_offset):
    devices = lax.axis_size(("panel", "slab"))
    blocks = stencil.shape[0]
    block_size = stencil.shape[1]
    cell_count = stencil.shape[2]
    pair_count = near_offset.shape[1]
    capacity = 2 * blocks // devices
    row_count = GRID // devices
    tile_rows = row_count // TILE
    tile_cols = GRID // TILE
    tile_total = tile_rows * tile_cols
    destination = block_dest[:, 0]
    one_hot = (destination[:, None] == jnp.arange(devices, dtype=jnp.int32)[None, :]).astype(
        jnp.int32
    )
    earlier = jnp.cumsum(one_hot, axis=0) - one_hot
    slot_index = destination * capacity + jnp.sum(earlier * one_hot, axis=1)
    tile_ids = (
        jnp.full((devices * capacity,), -1.0, jnp.float32)
        .at[slot_index]
        .set(block_tile.astype(jnp.float32))
    )

    def regroup(stacked):
        return lax.all_to_all(stacked, ("panel", "slab"), split_axis=2, concat_axis=2, tiled=True)

    def far_field(values):
        tile_values = jnp.einsum("bp,bpt->bt", values, stencil, preferred_element_type=jnp.float32)
        outgoing = (
            jnp.zeros((devices * capacity, cell_count), jnp.float32).at[slot_index].set(tile_values)
        )
        arrived, arrived_ids = (
            lax.all_to_all(
                outgoing.reshape(devices, capacity, cell_count),
                ("panel", "slab"),
                split_axis=0,
                concat_axis=0,
                tiled=True,
            ),
            lax.all_to_all(
                tile_ids.reshape(devices, capacity),
                ("panel", "slab"),
                split_axis=0,
                concat_axis=0,
                tiled=True,
            ),
        )
        where_ids = arrived_ids.reshape(-1)
        owned_tile = jnp.where(where_ids < 0.0, tile_total, where_ids.astype(jnp.int32))
        tile_sums = (
            jnp.zeros((tile_total, cell_count), jnp.float32)
            .at[owned_tile]
            .add(arrived.reshape(-1, cell_count), mode="drop")
        )
        grid_cells = (
            tile_sums.reshape(tile_rows, tile_cols, TILE, TILE)
            .transpose(0, 2, 1, 3)
            .reshape(row_count, GRID)
        )
        field = convolve(grid_cells, green, devices, regroup)
        back_tiles = field.reshape(tile_rows, TILE, tile_cols, TILE).transpose(0, 2, 1, 3)
        back_tiles = back_tiles.reshape(tile_total, cell_count).astype(jnp.bfloat16)
        returning = jnp.take(back_tiles, jnp.minimum(owned_tile, tile_total - 1), axis=0)
        returned = lax.all_to_all(
            returning.reshape(devices, capacity, cell_count),
            ("panel", "slab"),
            split_axis=0,
            concat_axis=0,
            tiled=True,
        )
        own_tiles = returned.reshape(devices * capacity, cell_count)[slot_index]
        return jnp.einsum("bpt,bt->bp", stencil, own_tiles, preferred_element_type=jnp.float32)

    couple = near_matrix.reshape(blocks, pair_count, block_size, block_size)
    positions = jnp.arange(blocks, dtype=jnp.int32)[:, None] + REACH + near_offset
    charge_blocks = charges.reshape(blocks, block_size)
    extended = extended_2(charge_blocks, ((("panel", "slab"), 0),), REACH)
    potentials = far_field(charge_blocks) + jnp.einsum(
        "bkps,bks->bp", couple, extended[positions], preferred_element_type=jnp.float32
    )
    residual = (potentials - target.reshape(blocks, block_size)).astype(jnp.bfloat16)
    terms = jnp.einsum("bkps,bp->bks", couple, residual, preferred_element_type=jnp.float32)
    extended = jnp.zeros((blocks + 2 * REACH, block_size), jnp.float32)
    extended = extended.at[positions.reshape(-1)].add(terms.reshape(-1, block_size))
    rims = jnp.concatenate([extended[:REACH], extended[blocks + REACH :]], axis=0)
    neighbour = extended_2(rims, ((("panel", "slab"), 0),), REACH)
    own_part = extended[REACH : blocks + REACH]
    own_part = own_part.at[:REACH].add(neighbour[:REACH])
    gradient = far_field(residual) + own_part.at[blocks - REACH :].add(neighbour[3 * REACH :])
    return (potentials.reshape(-1), gradient.reshape(-1))


def solution(mesh):
    return jax.shard_map(
        local,
        mesh=mesh,
        in_specs=(
            P(("panel", "slab")),
            P(("panel", "slab")),
            P(("panel", "slab"), None, None),
            P(("panel", "slab"), None, None),
            P(None, ("panel", "slab")),
            P(("panel", "slab"), None),
            P(("panel", "slab")),
            P(("panel", "slab"), None),
        ),
        out_specs=(P(("panel", "slab")), P(("panel", "slab"))),
        check_vma=False,
    )
```

profile of v0, /device:TPU:1, one launch (start us, length us, event | category | flops | bytes accessed | tf_op | source)
XLA Modules:
  0.0 347.5 jit_solution(201239427642557490)
XLA Ops:
  5.4 11.5 %all-to-all-start = ((f32[128,1,2]{2,1,0:T(1,128)}), f32[128,1,2]{2,1,0:T(1,128)S(1)}, u32[]{:S(2)}, u32[]{:S(2)}) async-start(f32[128,1,2]{2,1,0:T(1,128)} %bitcast.3), calls=%async_computation | async-start | bytes 131072 | tf_op jit(solution)/shard_map/all_to_all | solution.py:126
  17.7 2.8 fusion.335
  22.6 3.9 %all-to-all-done = f32[128,1,2]{2,1,0:T(1,128)S(1)} async-done(((f32[128,1,2]{2,1,0:T(1,128)}), f32[128,1,2]{2,1,0:T(1,128)S(1)}, u32[]{:S(2)}, u32[]{:S(2)}) %all-to-all-start) | async-done | bytes 1056 | tf_op jit(solution)/shard_map/all_to_all | solution.py:126
  26.5 5.8 %all-to-all-start.1 = ((f32[128,2,256]{2,1,0:T(2,128)}), f32[128,2,256]{2,1,0:T(2,128)S(1)}, u32[]{:S(2)}, u32[]{:S(2)}) async-start(f32[128,2,256]{2,1,0:T(2,128)} %reshape.321), calls=%async_computation.1 | async-start | bytes 524288 | tf_op jit(solution)/shard_map/all_to_all | solution.py:119
  33.0 10.4 %all-to-all-done.1 = f32[128,2,256]{2,1,0:T(2,128)S(1)} async-done(((f32[128,2,256]{2,1,0:T(2,128)}), f32[128,2,256]{2,1,0:T(2,128)S(1)}, u32[]{:S(2)}, u32[]{:S(2)}) %all-to-all-start.1) | async-done | bytes 262176 | tf_op jit(solution)/shard_map/all_to_all | solution.py:119
  49.0 3.2 reshape_reshape.6
  56.5 4.4 %copy.59 = f32[2,32,128,32]{3,1,0,2:T(8,128)} copy(f32[2,32,128,32]{2,3,1,0:T(8,128)S(1)} %pad_maximum_fusion.1) | data formatting | bytes 2097152 | tf_op jit(solution)/shard_map/stack | solution.py:45
  60.9 4.7 %reshape.479 = f32[128,1,2048]{2,1,0:T(1,128)} reshape(f32[128,2,32,32]{3,2,1,0:T(8,128)} %bitcast.280) | data formatting | bytes 2097152
  65.7 4.1 %all-to-all-start.2 = ((f32[128,1,2048]{2,1,0:T(1,128)}), f32[128,1,2048]{2,1,0:T(1,128)S(1)}, u32[]{:S(2)}, u32[]{:S(2)}) async-start(f32[128,1,2048]{2,1,0:T(1,128)} %reshape.479), calls=%async_computation.2 | async-start | bytes 2097152 | tf_op jit(solution)/shard_map/all_to_all | solution.py:111
  69.9 3.3 collective-permute-start
  73.3 4.0 %collective-permute-start.1 = (bf16[8,64]{1,0:T(8,128)(2,1)S(1)}, bf16[8,64]{1,0:T(8,128)(2,1)S(1)}, u32[]{:S(2)}, u32[]{:S(2)}) collective-permute-start(bf16[8,64]{1,0:T(8,128)(2,1)S(1)} %slice.247), channel_id=1, source_target_pairs={{1,0},{2,1},{3,2},{4,3},{5,4},{6,5},{7,6},{8,7},{9,8},{10,9},{11,1... | collective-permute-start | bytes 3080 | tf_op jit(solution)/shard_map/ppermute | solution.py:26
  77.5 11.7 %all-to-all-done.2 = f32[128,1,2048]{2,1,0:T(1,128)S(1)} async-done(((f32[128,1,2048]{2,1,0:T(1,128)}), f32[128,1,2048]{2,1,0:T(1,128)S(1)}, u32[]{:S(2)}, u32[]{:S(2)}) %all-to-all-start.2) | async-done | bytes 1048608 | tf_op jit(solution)/shard_map/all_to_all | solution.py:111
  89.7 3.2 reduce.12
  95.6 3.7 %copy.60 = f32[2,32,128,32]{2,3,1,0:T(8,128)S(1)} copy(f32[2,32,128,32]{3,1,0,2:T(8,128)} %bitcast.281) | data formatting | bytes 2097152 | tf_op jit(solution)/shard_map/all_to_all | solution.py:111
  112.4 4.4 %copy.66 = f32[2,32,128,32]{3,1,0,2:T(8,128)} copy(f32[2,32,128,32]{2,3,1,0:T(8,128)S(1)} %pad_maximum_fusion.4) | data formatting | bytes 2097152 | tf_op jit(solution)/shard_map/stack | solution.py:45
  116.9 4.7 %reshape.481 = f32[128,1,2048]{2,1,0:T(1,128)} reshape(f32[128,2,32,32]{3,2,1,0:T(8,128)} %bitcast.282) | data formatting | bytes 2097152
  121.5 3.9 %all-to-all-start.3 = ((f32[128,1,2048]{2,1,0:T(1,128)}), f32[128,1,2048]{2,1,0:T(1,128)S(1)}, u32[]{:S(2)}, u32[]{:S(2)}) async-start(f32[128,1,2048]{2,1,0:T(1,128)} %reshape.481), calls=%async_computation.3 | async-start | bytes 2097152 | tf_op jit(solution)/shard_map/all_to_all | solution.py:111
  125.8 7.8 %copy.72 = bf16[128,4,4096]{0,2,1:T(8,128)(2,1)} copy(bf16[128,4,4096]{2,1,0:T(4,128)(2,1)} %param.17) | data formatting | bytes 8388608 | tf_op args[3]
  133.6 13.0 %copy.106 = bf16[128,4,64,64]{3,2,1,0:T(8,128)(2,1)} copy(bf16[128,4,64,64]{0,3,2,1:T(8,128)(2,1)} %bitcast.288) | data formatting | bytes 8388608 | tf_op jit(solution)/shard_map/reshape | solution.py:160
  148.4 3.2 reduce.13
  151.6 2.7 reshape.482
  154.3 3.7 %copy.67 = f32[2,32,128,32]{2,3,1,0:T(8,128)S(1)} copy(f32[2,32,128,32]{3,1,0,2:T(8,128)} %bitcast.283) | data formatting | bytes 2097152 | tf_op jit(solution)/shard_map/all_to_all | solution.py:111
  166.5 9.8 %all-to-all-start.4 = ((bf16[128,2,256]{2,1,0:T(2,128)(2,1)}), bf16[128,2,256]{2,1,0:T(2,128)(2,1)S(1)}, u32[]{:S(2)}, u32[]{:S(2)}) async-start(bf16[128,2,256]{2,1,0:T(2,128)(2,1)} %reshape.324), calls=%async_computation.4 | async-start | bytes 262144 | tf_op jit(solution)/shard_map/all_to_all | solution.py:150
  176.4 5.6 %fusion.36 = f32[128,1,64,1]{2,1,3,0:T(1,128)S(1)} fusion(bf16[128,4,64,64]{3,2,1,0:T(8,128)(2,1)} %copy.106, bf16[128,4,64,1]{2,1,0,3:T(4,128)(2,1)S(1)} %bitcast.309), kind=kOutput, calls=%fused_computation.121 | convolution fusion | flops 4194304 | bytes 4292608 | tf_op jit(solution)/shard_map/bkps,bks->bp/dot_general | solution.py:164
  182.0 4.2 %all-to-all-done.4 = bf16[128,2,256]{2,1,0:T(2,128)(2,1)S(1)} async-done(((bf16[128,2,256]{2,1,0:T(2,128)(2,1)}), bf16[128,2,256]{2,1,0:T(2,128)(2,1)S(1)}, u32[]{:S(2)}, u32[]{:S(2)}) %all-to-all-start.4) | async-done | bytes 131104 | tf_op jit(solution)/shard_map/all_to_all | solution.py:150
  187.1 3.5 %fusion.65 = f32[128,1,64]{2,1,0:T(1,128)S(1)} fusion(bf16[128,64,256]{2,1,0:T(8,128)(2,1)} %param.16, bf16[128,256,1]{1,0,2:T(8,128)(2,1)S(1)} %bitcast.314), kind=kOutput, calls=%fused_computation.143 | convolution fusion | flops 4194304 | bytes 4292608 | tf_op jit(solution)/shard_map/bpt,bt->bp/dot_general | solution.py:158
  192.6 16.4 %all_to_all.50 = f32[128,2,256]{2,1,0:T(2,128)S(1)} all-to-all(f32[128,2,256]{2,1,0:T(2,128)S(1)} %reshape.329), channel_id=1, replica_groups=mesh['panel'=32,'slab'=4] {'panel','slab'}, dimensions={0} | all-to-all | bytes 524288 | tf_op jit(solution)/shard_map/all_to_all | solution.py:119
  211.8 3.0 copy.74
  214.8 3.2 reshape_reshape.7
  222.3 4.4 %copy.75 = f32[2,32,128,32]{3,1,0,2:T(8,128)} copy(f32[2,32,128,32]{2,3,1,0:T(8,128)S(1)} %pad_maximum_fusion.6) | data formatting | bytes 2097152 | tf_op jit(solution)/shard_map/stack | solution.py:45
  226.7 4.7 %reshape.483 = f32[128,1,2048]{2,1,0:T(1,128)} reshape(f32[128,2,32,32]{3,2,1,0:T(8,128)} %bitcast.284) | data formatting | bytes 2097152
  231.4 4.2 %all-to-all-start.6 = ((f32[128,1,2048]{2,1,0:T(1,128)}), f32[128,1,2048]{2,1,0:T(1,128)S(1)}, u32[]{:S(2)}, u32[]{:S(2)}) async-start(f32[128,1,2048]{2,1,0:T(1,128)} %reshape.483), calls=%async_computation.6 | async-start | bytes 2097152 | tf_op jit(solution)/shard_map/all_to_all | solution.py:111
  235.8 19.2 %all-to-all-done.6 = f32[128,1,2048]{2,1,0:T(1,128)S(1)} async-done(((f32[128,1,2048]{2,1,0:T(1,128)}), f32[128,1,2048]{2,1,0:T(1,128)S(1)}, u32[]{:S(2)}, u32[]{:S(2)}) %all-to-all-start.6) | async-done | bytes 1048608 | tf_op jit(solution)/shard_map/all_to_all | solution.py:111
  254.9 3.2 reduce.14
  260.8 3.9 %copy.76 = f32[2,32,128,32]{2,3,1,0:T(8,128)S(1)} copy(f32[2,32,128,32]{3,1,0,2:T(8,128)} %bitcast.285) | data formatting | bytes 2097152 | tf_op jit(solution)/shard_map/all_to_all | solution.py:111
  277.8 4.4 %copy.82 = f32[2,32,128,32]{3,1,0,2:T(8,128)} copy(f32[2,32,128,32]{2,3,1,0:T(8,128)S(1)} %pad_maximum_fusion.9) | data formatting | bytes 2097152 | tf_op jit(solution)/shard_map/stack | solution.py:45
  282.3 4.7 %reshape.485 = f32[128,1,2048]{2,1,0:T(1,128)} reshape(f32[128,2,32,32]{3,2,1,0:T(8,128)} %bitcast.286) | data formatting | bytes 2097152
  287.0 3.9 %all-to-all-start.7 = ((f32[128,1,2048]{2,1,0:T(1,128)}), f32[128,1,2048]{2,1,0:T(1,128)S(1)}, u32[]{:S(2)}, u32[]{:S(2)}) async-start(f32[128,1,2048]{2,1,0:T(1,128)} %reshape.485), calls=%async_computation.7 | async-start | bytes 2097152 | tf_op jit(solution)/shard_map/all_to_all | solution.py:111
  290.9 4.6 %fusion.89 = f32[128,1,4,64]{3,1,2,0:T(1,128)S(1)} fusion(bf16[128,4,64,64]{3,2,1,0:T(8,128)(2,1)} %copy.106, bf16[128,64,1,1]{1,0,2,3:T(8,128)(2,1)S(1)} %bitcast.302), kind=kOutput, calls=%fused_computation.172 | convolution fusion | flops 4194304 | bytes 4341760 | tf_op jit(solution)/shard_map/bkps,bp->bks/dot_general | solution.py:168
  297.7 3.3 collective-permute-start.2
  301.0 3.5 %collective-permute-start.3 = (f32[8,64]{1,0:T(8,128)S(1)}, f32[8,64]{1,0:T(8,128)S(1)}, u32[]{:S(2)}, u32[]{:S(2)}) collective-permute-start(f32[8,64]{1,0:T(8,128)S(1)} %get-tuple-element.57), channel_id=1, source_target_pairs={{1,0},{2,1},{3,2},{4,3},{5,4},{6,5},{7,6},{8,7},{9,8},{10,9},{11,1... | collective-permute-start | bytes 6152 | tf_op jit(solution)/shard_map/ppermute | solution.py:26
  305.2 5.0 %all-to-all-done.7 = f32[128,1,2048]{2,1,0:T(1,128)S(1)} async-done(((f32[128,1,2048]{2,1,0:T(1,128)}), f32[128,1,2048]{2,1,0:T(1,128)S(1)}, u32[]{:S(2)}, u32[]{:S(2)}) %all-to-all-start.7) | async-done | bytes 1048608 | tf_op jit(solution)/shard_map/all_to_all | solution.py:111
  310.2 3.1 reduce.15
  313.4 3.0 reshape.486
  316.3 3.7 %copy.83 = f32[2,32,128,32]{2,3,1,0:T(8,128)S(1)} copy(f32[2,32,128,32]{3,1,0,2:T(8,128)} %bitcast.287) | data formatting | bytes 2097152 | tf_op jit(solution)/shard_map/all_to_all | solution.py:111
  328.3 3.9 %all-to-all-start.8 = ((bf16[128,2,256]{2,1,0:T(2,128)(2,1)}), bf16[128,2,256]{2,1,0:T(2,128)(2,1)S(1)}, u32[]{:S(2)}, u32[]{:S(2)}) async-start(bf16[128,2,256]{2,1,0:T(2,128)(2,1)} %reshape.332), calls=%async_computation.8 | async-start | bytes 262144 | tf_op jit(solution)/shard_map/all_to_all | solution.py:150
  332.3 9.8 %all-to-all-done.8 = bf16[128,2,256]{2,1,0:T(2,128)(2,1)S(1)} async-done(((bf16[128,2,256]{2,1,0:T(2,128)(2,1)}), bf16[128,2,256]{2,1,0:T(2,128)(2,1)S(1)}, u32[]{:S(2)}, u32[]{:S(2)}) %all-to-all-start.8) | async-done | bytes 131104 | tf_op jit(solution)/shard_map/all_to_all | solution.py:150
  343.0 3.4 fusion.62
  (146 shorter events, 83.4 us)
Async XLA Ops:
  5.4 21.1 %all-to-all-start = ((f32[128,1,2]{2,1,0:T(1,128)}), f32[128,1,2]{2,1,0:T(1,128)S(1)}, u32[]{:S(2)}, u32[]{:S(2)}) async-start(f32[128,1,2]{2,1,0:T(1,128)} %bitcast.3), calls=%async_computation | async-start | bytes 131072 | tf_op jit(solution)/shard_map/all_to_all | solution.py:126
  26.5 16.9 %all-to-all-start.1 = ((f32[128,2,256]{2,1,0:T(2,128)}), f32[128,2,256]{2,1,0:T(2,128)S(1)}, u32[]{:S(2)}, u32[]{:S(2)}) async-start(f32[128,2,256]{2,1,0:T(2,128)} %reshape.321), calls=%async_computation.1 | async-start | bytes 524288 | tf_op jit(solution)/shard_map/all_to_all | solution.py:119
  60.9 8.9 %copy-start.2 = (bf16[8192]{0:T(1024)(128)(2,1)S(1)}, bf16[8192]{0:T(1024)(128)(2,1)}, u32[]{:S(2)}) copy-start(bf16[8192]{0:T(1024)(128)(2,1)} %param.14) | copy-start | bytes 49156
  60.9 16.4 %copy-start.1 = (f32[4096,32]{0,1:T(8,128)S(1)}, f32[4096,32]{0,1:T(8,128)}, u32[]{:S(2)}) copy-start(f32[4096,32]{0,1:T(8,128)} %param.18) | copy-start | bytes 1572868
  65.7 23.5 %all-to-all-start.2 = ((f32[128,1,2048]{2,1,0:T(1,128)}), f32[128,1,2048]{2,1,0:T(1,128)S(1)}, u32[]{:S(2)}, u32[]{:S(2)}) async-start(f32[128,1,2048]{2,1,0:T(1,128)} %reshape.479), calls=%async_computation.2 | async-start | bytes 2097152 | tf_op jit(solution)/shard_map/all_to_all | solution.py:111
  69.9 77.1 %collective-permute-start = (bf16[8,64]{1,0:T(8,128)(2,1)S(1)}, bf16[8,64]{1,0:T(8,128)(2,1)S(1)}, u32[]{:S(2)}, u32[]{:S(2)}) collective-permute-start(bf16[8,64]{1,0:T(8,128)(2,1)S(1)} %slice.245), channel_id=1, source_target_pairs={{0,1},{1,2},{2,3},{3,4},{4,5},{5,6},{6,7},{7,8},{8,9},{9,10},{10,1... | collective-permute-start | bytes 3080 | tf_op jit(solution)/shard_map/ppermute | solution.py:24
  73.3 73.7 %collective-permute-start.1 = (bf16[8,64]{1,0:T(8,128)(2,1)S(1)}, bf16[8,64]{1,0:T(8,128)(2,1)S(1)}, u32[]{:S(2)}, u32[]{:S(2)}) collective-permute-start(bf16[8,64]{1,0:T(8,128)(2,1)S(1)} %slice.247), channel_id=1, source_target_pairs={{1,0},{2,1},{3,2},{4,3},{5,4},{6,5},{7,6},{8,7},{9,8},{10,9},{11,1... | collective-permute-start | bytes 3080 | tf_op jit(solution)/shard_map/ppermute | solution.py:26
  116.9 8.6 %copy-start.4 = (s32[128,4]{0,1:T(4,128)S(1)}, s32[128,4]{0,1:T(4,128)}, u32[]{:S(2)}) copy-start(s32[128,4]{0,1:T(4,128)} %param.21) | copy-start | bytes 6148
  121.5 26.9 %all-to-all-start.3 = ((f32[128,1,2048]{2,1,0:T(1,128)}), f32[128,1,2048]{2,1,0:T(1,128)S(1)}, u32[]{:S(2)}, u32[]{:S(2)}) async-start(f32[128,1,2048]{2,1,0:T(1,128)} %reshape.481), calls=%async_computation.3 | async-start | bytes 2097152 | tf_op jit(solution)/shard_map/all_to_all | solution.py:111
  133.6 13.0 %copy-start.3 = (f32[8192]{0:T(1024)S(1)}, f32[8192]{0:T(1024)}, u32[]{:S(2)}) copy-start(f32[8192]{0:T(1024)} %param.15) | copy-start | bytes 98308
  166.5 19.6 %all-to-all-start.4 = ((bf16[128,2,256]{2,1,0:T(2,128)(2,1)}), bf16[128,2,256]{2,1,0:T(2,128)(2,1)S(1)}, u32[]{:S(2)}, u32[]{:S(2)}) async-start(bf16[128,2,256]{2,1,0:T(2,128)(2,1)} %reshape.324), calls=%async_computation.4 | async-start | bytes 262144 | tf_op jit(solution)/shard_map/all_to_all | solution.py:150
  187.1 3.6 %copy-start = (bf16[128,64,256]{2,1,0:T(8,128)(2,1)S(1)}, bf16[128,64,256]{2,1,0:T(8,128)(2,1)}, u32[]{:S(2)}) copy-start(bf16[128,64,256]{2,1,0:T(8,128)(2,1)} %param.16) | copy-start | bytes 12582916
  231.4 23.6 %all-to-all-start.6 = ((f32[128,1,2048]{2,1,0:T(1,128)}), f32[128,1,2048]{2,1,0:T(1,128)S(1)}, u32[]{:S(2)}, u32[]{:S(2)}) async-start(f32[128,1,2048]{2,1,0:T(1,128)} %reshape.483), calls=%async_computation.6 | async-start | bytes 2097152 | tf_op jit(solution)/shard_map/all_to_all | solution.py:111
  287.0 23.3 %all-to-all-start.7 = ((f32[128,1,2048]{2,1,0:T(1,128)}), f32[128,1,2048]{2,1,0:T(1,128)S(1)}, u32[]{:S(2)}, u32[]{:S(2)}) async-start(f32[128,1,2048]{2,1,0:T(1,128)} %reshape.485), calls=%async_computation.7 | async-start | bytes 2097152 | tf_op jit(solution)/shard_map/all_to_all | solution.py:111
  297.7 7.5 %collective-permute-start.2 = (f32[8,64]{1,0:T(8,128)S(1)}, f32[8,64]{1,0:T(8,128)S(1)}, u32[]{:S(2)}, u32[]{:S(2)}) collective-permute-start(f32[8,64]{1,0:T(8,128)S(1)} %get-tuple-element.58), channel_id=1, source_target_pairs={{0,1},{1,2},{2,3},{3,4},{4,5},{5,6},{6,7},{7,8},{8,9},{9,10},{10,1... | collective-permute-start | bytes 6152 | tf_op jit(solution)/shard_map/ppermute | solution.py:24
  301.0 31.2 %collective-permute-start.3 = (f32[8,64]{1,0:T(8,128)S(1)}, f32[8,64]{1,0:T(8,128)S(1)}, u32[]{:S(2)}, u32[]{:S(2)}) collective-permute-start(f32[8,64]{1,0:T(8,128)S(1)} %get-tuple-element.57), channel_id=1, source_target_pairs={{1,0},{2,1},{3,2},{4,3},{5,4},{6,5},{7,6},{8,7},{9,8},{10,9},{11,1... | collective-permute-start | bytes 6152 | tf_op jit(solution)/shard_map/ppermute | solution.py:26
  328.3 13.8 %all-to-all-start.8 = ((bf16[128,2,256]{2,1,0:T(2,128)(2,1)}), bf16[128,2,256]{2,1,0:T(2,128)(2,1)S(1)}, u32[]{:S(2)}, u32[]{:S(2)}) async-start(bf16[128,2,256]{2,1,0:T(2,128)(2,1)} %reshape.332), calls=%async_computation.8 | async-start | bytes 262144 | tf_op jit(solution)/shard_map/all_to_all | solution.py:150
where the time goes:
time: 353 us; the launch traced here: 348 us
  local copies, waits for them, and re-layouts  120 us (34%)
  waiting for transfers between devices  64.2 us (18%)
  starting transfers between devices  61.2 us (17%)
  matrix products  57.3 us (16%)
  other arithmetic  26.2 us (7%)
  blocking collectives  16.4 us (5%)
    unnamed x22, local copies, waits for them, and re-layouts  37.9 us
    all_to_all x4, waiting for transfers between devices, regroup(): lax.all_to_all(stacked, ('panel', 'slab'), split_axis=2, concat_axis=2, t...  35.9 us
    another operation x4, local copies, waits for them, and re-layouts, rotate(): return jnp.stack([with_cos[0] - with_sin[1], with_sin[0] + with_cos[1]])  17.8 us
    all_to_all x1, blocking collectives, far_field(): lax.all_to_all(outgoing.reshape(devices, capacity, cell_count), ('panel',...  16.4 us
    all_to_all x4, starting transfers between devices, regroup(): lax.all_to_all(stacked, ('panel', 'slab'), split_axis=2, concat_axis=2, t...  16.1 us
    dot_general x12, matrix products, rotate(): with_sin = jnp.einsum(formula, stacked, sine, precision=HIGHEST)  15.8 us
    all_to_all x5, local copies, waits for them, and re-layouts, regroup(): lax.all_to_all(stacked, ('panel', 'slab'), split_axis=2, concat_axis=2, t...  15.6 us
    dot_general x12, matrix products, rotate(): with_cos = jnp.einsum(formula, stacked, cosine, precision=HIGHEST)  15.3 us
  transfers between devices with their start and end apart: 12, of which 7 were waited for; matrix products, arithmetic and copies ran while one was open for 27% of the time, Pallas kernels for 0%

commit v1 on v0

v1 whole, which is shorter than its diff:
```python
import functools
import math

import jax
import jax.numpy as jnp
import numpy as np
from jax import lax
from jax.experimental import pallas as pl
from jax.experimental.pallas import tpu as pltpu
from jax.sharding import PartitionSpec as P

GRID = 4096
TILE = 16
REACH = 8
NDEV = 128
SLABS = 4
BLOCKS = 128
PANEL = 64
CELLS = 256
LANES = 128
MSG = 8
ROWS = NDEV * MSG
MESH = pl.DeviceIdType.MESH
F32 = jnp.float32
BF16 = jnp.bfloat16
TABLES = ("w1", "w2", "m0", "m0i", "a1", "w3", "t2", "t1", "tm")


def make_tables():
    def angle(rows, cols, modulus):
        return 2.0 * math.pi / modulus * ((np.outer(rows, cols)) % modulus)

    out = {}
    th = angle(np.arange(128), np.arange(256), 256)
    w1 = np.concatenate([np.cos(th), -np.sin(th)], 0)
    w1[128] = (-1.0) ** np.arange(256)
    out["w1"] = w1
    th = angle(np.arange(16), np.arange(16), 16)
    c, s = np.kron(np.eye(8), np.cos(th)), np.kron(np.eye(8), np.sin(th))
    out["w2"] = np.concatenate([c, s], 1)
    m0 = np.zeros((2, 16, 2, 16))
    idx = np.arange(16)
    m0[0, :, 0, 0] = 1.0
    m0[0, :, 1, 0] = (-1.0) ** idx
    for k in range(1, 8):
        t = 2 * math.pi * ((idx * k) % 16) / 16
        m0[0, :, 0, k], m0[0, :, 1, k] = np.cos(t), -np.sin(t)
    for n in range(8):
        t = 2 * math.pi * ((idx * (1 + 2 * n)) % 32) / 32
        m0[1, :, 0, 8 + n], m0[1, :, 1, 8 + n] = np.cos(t), -np.sin(t)
    big = np.zeros((2, 8, 16, 2, 8, 16))
    for a in range(8):
        big[:, a, :, :, a, :] = m0
    out["m0"] = big.reshape(256, 256)
    inv = m0.copy()
    inv[:, :, :, 0] *= 0.5
    big = np.zeros((2, 8, 16, 2, 8, 16))
    for a in range(8):
        big[:, a, :, :, a, :] = inv
    out["m0i"] = big.reshape(256, 256).T
    th = angle(np.arange(128), np.arange(128), 128)
    out["a1"] = np.concatenate([np.cos(th), np.sin(th)], 1)
    th = angle(np.arange(8), np.arange(8), 8)
    out["w3"] = np.concatenate([np.kron(np.cos(th), np.eye(16)), np.kron(np.sin(th), np.eye(16))], 1)
    th = np.tile(angle(np.arange(128), np.arange(16), GRID), (1, 8))
    th[0] = 0.0
    out["t2"] = np.concatenate([np.cos(th), np.sin(th)], 1)
    th = np.repeat(angle(np.arange(128), np.arange(32), GRID), 16, axis=1)
    out["t1"] = np.concatenate([np.cos(th), np.sin(th)], 1)
    th = np.repeat(angle(np.arange(4), np.arange(8), 32), 16, axis=1)
    tm = np.zeros((8, 256))
    tm[:4] = np.concatenate([np.cos(th), np.sin(th)], 1)
    out["tm"] = tm
    return {k: np.asarray(v, np.float32) for k, v in out.items()}


def dot(a, b):
    return lax.dot_general(a, b, (((1,), (0,)), ((), ())), preferred_element_type=F32)


def dot_nt(a, b):
    return lax.dot_general(a, b, (((1,), (1,)), ((), ())), preferred_element_type=F32)


def split(x):
    hi = x.astype(BF16)
    return hi, (x - hi.astype(F32)).astype(BF16)


def dot3(a, b):
    return dot(a[0], b[0]) + (dot(a[0], b[1]) + dot(a[1], b[0]))


def iota(shape, dim):
    return lax.broadcasted_iota(jnp.int32, shape, dim)


def cat(parts, axis):
    return jnp.concatenate(parts, axis=axis)


def kernel(
    q_ref, near_ref, target_ref, stencil_hbm, green_ref, dest_ref, tile_ref,
    w1_ref, w2_ref, m0_ref, m0i_ref, a1_ref, w3_ref, t2_ref, t1_ref, tm_ref,
    pot_ref, res_ref, far_ref,
    stencil, sbuf, rbuf, gsend, grecv, ga, gb, val, tv, wf, wi, mats,
    send_sem, recv_sem, gsend_sem, grecv_sem, load_sem,
):
    panel = lax.axis_index("panel")
    slab = lax.axis_index("slab")
    me = panel * SLABS + slab
    pz, px, pc = panel // 8, (panel // 2) % 4, panel % 2

    load = pltpu.make_async_copy(stencil_hbm, stencil, load_sem)
    load.start()

    def peer_panel(i):
        return ((pz + 2 + i // 8) % 4) * 8 + ((px + 2 + (i // 2) % 4) % 4) * 2 + (pc + i % 2) % 2

    own = 20

    barrier = pltpu.get_barrier_semaphore()

    def greet(i, carry):
        other = peer_panel(i)
        for dy in (2, 3, 1):
            pl.semaphore_signal(barrier, inc=1, device_id=(other, (slab + dy) % 4), device_id_type=MESH)

        @pl.when(i != own)
        def _():
            pl.semaphore_signal(barrier, inc=1, device_id=(other, slab), device_id_type=MESH)

        return carry

    lax.fori_loop(0, 32, greet, 0)

    def pair(slot, value):
        hi, lo = split(value)
        mats[2 * slot] = hi
        mats[2 * slot + 1] = lo

    def mat(slot):
        return mats[2 * slot], mats[2 * slot + 1]

    def circle(ref):
        return ref[:, :LANES], ref[:, LANES:]

    pair(0, w1_ref[...])
    c, s = circle(w2_ref)
    pair(1, cat([cat([c, -s], 1), cat([s, c], 1)], 0))
    pair(2, cat([cat([c, s], 1), cat([-s, c], 1)], 0))
    pair(3, m0_ref[...])
    pair(4, m0i_ref[...])
    c, s = circle(a1_ref)
    pair(5, cat([cat([c, s], 1), cat([-s, c], 1)], 0))
    pair(6, cat([cat([c, -s], 1), cat([s, c], 1)], 0))
    c, s = circle(w3_ref)
    pair(7, cat([cat([c, -s], 1), cat([s, c], 1)], 0))
    pair(8, cat([cat([c, s], 1), cat([-s, c], 1)], 0))

    rows128, lanes128 = iota((128, 128), 0), iota((128, 128), 1)
    dest_row = dest_ref[...]
    tile_row = tile_ref[...]

    def column(row):
        return jnp.sum(jnp.where(rows128 == lanes128, row, 0), axis=1, keepdims=True)

    dest_col = column(dest_row)
    same = dest_col == dest_row
    rank_row = jnp.sum(jnp.where(same & (rows128 < lanes128), 1, 0), axis=0, keepdims=True)
    rank_col = jnp.sum(jnp.where(same & (lanes128 < rows128), 1, 0), axis=1, keepdims=True)
    one, zero = F32(1.0), F32(0.0)
    out_pick = cat(
        [jnp.where((dest_row == rows128) & (rank_row == k), one, zero) for k in range(2)], 0
    )
    in_pick = cat(
        [jnp.where((dest_col == lanes128) & (rank_col == k), one, zero) for k in range(2)], 1
    ).astype(BF16)
    ids = jnp.sum(out_pick * (tile_row + 1).astype(F32), axis=1, keepdims=True)
    id_rows = jnp.where(lanes128 == 0, ids[:128], jnp.where(lanes128 == 1, ids[128:], 0.0))
    out_pick = out_pick.astype(BF16)

    def exchange(step):
        src, dst = sbuf.at[step], rbuf.at[step]
        mine = pl.ds(pl.multiple_of(me * MSG, MSG), MSG)

        def send(other, other_slab):
            theirs = pl.ds(pl.multiple_of((other * SLABS + other_slab) * MSG, MSG), MSG)
            pltpu.make_async_remote_copy(
                src_ref=src.at[theirs],
                dst_ref=dst.at[mine],
                send_sem=send_sem.at[step],
                recv_sem=recv_sem.at[step],
                device_id=(other, other_slab),
                device_id_type=MESH,
            ).start()

        def body(i, carry):
            other = peer_panel(i)
            for dy in (2, 3, 1):
                send(other, (slab + dy) % 4)

            @pl.when(i != own)
            def _():
                send(other, slab)

            return carry

        lax.fori_loop(0, 32, body, 0)
        pltpu.make_async_copy(src.at[mine], dst.at[mine], recv_sem.at[step]).start()

    def arrived(step):
        pltpu.make_async_copy(sbuf.at[step], rbuf.at[step], recv_sem.at[step]).wait()

    def sent(step):
        part = pl.ds(0, ROWS - MSG)
        pltpu.make_async_copy(
            sbuf.at[step, part], rbuf.at[step, part], send_sem.at[step]
        ).wait()

    def put(step, row, value):
        sbuf[step, pl.ds(row, NDEV, stride=MSG), :] = value

    def get(step, row):
        return rbuf[step, pl.ds(row, NDEV, stride=MSG), :]

    def pack(kk, carry):
        gsend[pl.ds(kk, 32, stride=32), :] = green_ref[:, pl.ds(pl.multiple_of(kk * LANES, LANES), LANES)]
        return carry

    lax.fori_loop(0, 32, pack, 0)

    def green_copies():
        k2 = me // 8

        def body(j, carry):
            k1 = (me % 8) * 32 + j
            low = jnp.where(k1 < 128, 1, 0)
            is_mid = jnp.where(k1 == 128, 1, 0)
            is_zero = jnp.where(k1 == 0, 1, 0)
            high = 1 - low - is_mid
            target_dev = low * k1 + high * (256 - k1)
            upper = k2 // 8
            beyond = jnp.where(k2 > 8, 1, 0)
            slot_zero = (1 - upper) * k2 + upper * (1 - beyond) * 16 + beyond * (32 - k2)
            slot_mid = (1 - upper) * (8 + k2) + upper * (39 - k2)
            slot = (low - is_zero) * k2 + is_zero * slot_zero + is_mid * slot_mid + high * (31 - k2)
            src = gsend.at[pl.ds(pl.multiple_of(j * 32, 32), 32)]
            dst = grecv.at[pl.ds(pl.multiple_of(slot * 32, 32), 32)]

            @pl.when(target_dev != me)
            def _():
                pltpu.make_async_remote_copy(
                    src_ref=src, dst_ref=dst, send_sem=gsend_sem.at[j], recv_sem=grecv_sem,
                    device_id=(target_dev // SLABS, target_dev % SLABS), device_id_type=MESH,
                ).start()

            @pl.when(target_dev == me)
            def _():
                pltpu.make_async_copy(src, dst, grecv_sem).start()

            return carry

        lax.fori_loop(0, 32, body, 0)

    def green_sent():
        def body(j, carry):
            k1 = (me % 8) * 32 + j
            low = jnp.where(k1 < 128, 1, 0)
            high = jnp.where(k1 > 128, 1, 0)
            target_dev = low * k1 + high * (256 - k1)

            @pl.when(target_dev != me)
            def _():
                part = pl.ds(pl.multiple_of(j * 32, 32), 32)
                pltpu.make_async_copy(gsend.at[part], grecv.at[part], gsend_sem.at[j]).wait()

            return carry

        lax.fori_loop(0, 32, body, 0)

    def green_ready():
        pltpu.make_async_copy(gsend, grecv, grecv_sem).wait()
        scale = 2.0 ** -24
        flip = jnp.where((rows128 + lanes128 == 128) & (rows128 > 0), one, zero).astype(BF16)
        first = jnp.where((rows128 == 0) & (lanes128 == 0), one, zero).astype(BF16)
        eye = jnp.where(rows128 == lanes128, one, zero).astype(BF16)
        turn = cat([flip, first], 1)
        special = (lanes128 % 16 == 0) & (me == 0)

        def rows_of(base, kappa):
            return cat(
                [grecv[pl.ds(base * 32 + kappa(n), 16, stride=32), :] for n in range(8)], 0
            )

        for m in range(4):
            def plain(base):
                hi, lo = split(rows_of(base, lambda n: m + 4 * n))
                return dot_nt(eye, hi) + dot_nt(eye, lo)

            def turned(base):
                one_ = rows_of(base, lambda n: 31 - m - 4 * n)
                two_ = rows_of(base, lambda n: (32 - m - 4 * n) % 32)
                hi, lo = split(cat([one_, two_], 1))
                return dot_nt(turn, hi) + dot_nt(turn, lo)

            d, dr, o, orr = plain(0), turned(0), plain(16), turned(16)
            ga[:, m * LANES:(m + 1) * LANES] = (d + jnp.where(special, dr, orr)) * scale
            gb[:, m * LANES:(m + 1) * LANES] = (jnp.where(special, o, d) + orr) * scale

    lane64 = iota((128, 128), 1) // 64
    row16 = iota((128, 128), 0) % 16

    def project():
        v = val[...]
        spread = cat(
            [jnp.where(lane64 + 2 * i == row16, v, 0.0).astype(BF16) for i in range(8)], 1
        )
        for g in range(8):
            part = stencil[g * 1024:(g + 1) * 1024, :]
            tv[g * 16:(g + 1) * 16, :] = dot(spread[g * 16:(g + 1) * 16, :], part)
        hi, lo = split(tv[...])
        return dot(out_pick, hi) + dot(out_pick, lo)

    def interpolate(own_tiles):
        rows = []
        l64, r16 = iota((16, 128), 1) // 64, iota((16, 128), 0)
        for g in range(8):
            part = stencil[g * 1024:(g + 1) * 1024, :]
            r = dot_nt(own_tiles[g * 16:(g + 1) * 16, :], part)
            acc = jnp.zeros((16, 128), F32)
            for i in range(8):
                acc = acc + jnp.where(l64 + 2 * i == r16, r[:, i * LANES:(i + 1) * LANES], 0.0)
            rows.append(acc)
        far = cat(rows, 0)
        return far + pltpu.roll(far, 64, 1)

    def cmul(re, im, c, s):
        return re * c + im * s, im * c - re * s

    def cmul_conj(re, im, c, s):
        return re * c - im * s, im * c + re * s

    def lane_tile(x, j):
        return x[:, j * LANES:(j + 1) * LANES]

    head = iota((8, 128), 0) == 0

    def special_rows(parts, slot, outs):
        small = dot3(split(cat([p[:8] for p in parts], 0)), mat(slot))
        fixed = []
        for j in range(4):
            out = outs[j]
            h2 = iota((8, 256), 0) == 0
            fixed.append(cat([jnp.where(h2, small[8 * j:8 * j + 8], out[:8]), out[8:]], 0))
        return fixed

    def evaluate(step0, which):
        out = project()
        for k in range(2):
            for h in range(2):
                put(step0, 2 * k + h, lane_tile(out[128 * k:128 * k + 128], h))
        put(step0, 4, id_rows)

        @pl.when(which == 0)
        def _():
            pl.semaphore_wait(barrier, NDEV - 1)

        exchange(step0)

        @pl.when(which == 0)
        def _():
            green_copies()

        arrived(step0)

        @pl.when(which == 0)
        def _():
            idm = get(step0, 4)
            tc = iota((128, 256), 1)
            for tr in range(2):
                pick = cat(
                    [
                        jnp.where(idm[:, k:k + 1].astype(jnp.int32) == tc + (tr * 256 + 1), one, zero)
                        for k in range(2)
                    ],
                    0,
                ).astype(BF16)
                for t in range(2):
                    wf[2 * tr + t] = dot_nt(mats[t], pick).astype(BF16)
                    wi[t, :, tr * 256:(tr + 1) * 256] = dot_nt(pick, mats[t]).astype(BF16)

        tiles = split(
            cat([cat([get(step0, 2 * k + h) for h in range(2)], 1) for k in range(2)], 0)
        )
        c2, s2 = t2_ref[:, :LANES], t2_ref[:, LANES:]
        parts = []
        for tr in range(2):
            y = dot3((wf[2 * tr], wf[2 * tr + 1]), tiles)
            for h in range(2):
                re, im = cmul(lane_tile(y[:128], h), lane_tile(y[128:], h), c2, s2)
                parts.append(cat([re, im], 1))
        prod = dot3(split(cat(parts, 0)), mat(1))
        outs = special_rows(parts, 3, [prod[128 * j:128 * j + 128] for j in range(4)])
        for j in range(4):
            put(step0 + 1, j, outs[j][:, :LANES])
            put(step0 + 1, 4 + j, outs[j][:, LANES:])
        exchange(step0 + 1)

        @pl.when(which == 0)
        def _():
            green_ready()

        arrived(step0 + 1)
        x = cat(
            [
                cat([get(step0 + 1, j) for j in range(4)], 1),
                cat([get(step0 + 1, 4 + j) for j in range(4)], 1),
            ],
            0,
        )
        y = dot3(mat(5), split(x))
        re, im = cmul(y[:128], y[128:], t1_ref[:, :512], t1_ref[:, 512:])
        r = [lane_tile(re, j) for j in range(4)]
        i = [lane_tile(im, j) for j in range(4)]
        er, ei, dr, di = r[0] + r[2], i[0] + i[2], r[0] - r[2], i[0] - i[2]
        fr, fi, hr, hi_ = r[1] + r[3], i[1] + i[3], r[1] - r[3], i[1] - i[3]
        vs = [(er + fr, ei + fi), (dr + hi_, di - hr), (er - fr, ei - fi), (dr - hi_, di + hr)]
        parts = []
        for m in range(4):
            cm, sm = tm_ref[m:m + 1, :LANES], tm_ref[m:m + 1, LANES:]
            parts.append(cat(list(cmul(vs[m][0], vs[m][1], cm, sm)), 1))
        f = dot3(split(cat(parts, 0)), mat(7))
        both = []
        for g in (ga, gb):
            for m in range(4):
                gm = g[:, m * LANES:(m + 1) * LANES]
                fm = f[128 * m:128 * m + 128]
                both.append(cat([fm[:, :LANES] * gm, fm[:, LANES:] * gm], 1))
        p = dot3(split(cat(both, 0)), mat(8))
        stacked = []
        for e in range(2):
            vs = []
            for m in range(4):
                cm, sm = tm_ref[m:m + 1, :LANES], tm_ref[m:m + 1, LANES:]
                pm = p[512 * e + 128 * m:512 * e + 128 * m + 128]
                vs.append(cmul_conj(pm[:, :LANES], pm[:, LANES:], cm, sm))
            r = [v[0] for v in vs]
            i = [v[1] for v in vs]
            er, ei, dr, di = r[0] + r[2], i[0] + i[2], r[0] - r[2], i[0] - i[2]
            fr, fi, hr, hi_ = r[1] + r[3], i[1] + i[3], r[1] - r[3], i[1] - i[3]
            zs = [(er + fr, ei + fi), (dr - hi_, di + hr), (er - fr, ei - fi), (dr + hi_, di - hr)]
            re, im = cmul_conj(
                cat([z[0] for z in zs], 1), cat([z[1] for z in zs], 1),
                t1_ref[:, :512], t1_ref[:, 512:],
            )
            stacked.append(split(cat([re, im], 0)))
        inv = mat(6)
        yr = dot3((inv[0][:128], inv[1][:128]), stacked[0])
        yi = dot3((inv[0][128:], inv[1][128:]), stacked[1])
        for j in range(4):
            put(step0 + 2, j, lane_tile(yr, j))
            put(step0 + 2, 4 + j, lane_tile(yi, j))
        exchange(step0 + 2)
        arrived(step0 + 2)
        parts = [cat([get(step0 + 2, j), get(step0 + 2, 4 + j)], 1) for j in range(4)]
        prod = dot3(split(cat(parts, 0)), mat(2))
        outs = special_rows(parts, 4, [prod[128 * j:128 * j + 128] for j in range(4)])
        zs = [cmul_conj(o[:, :LANES], o[:, LANES:], c2, s2) for o in outs]
        y = cat(
            [
                cat([cat([zs[2 * tr][0], zs[2 * tr + 1][0]], 1), cat([zs[2 * tr][1], zs[2 * tr + 1][1]], 1)], 0)
                for tr in range(2)
            ],
            0,
        )
        back = dot3((wi[0], wi[1]), split(y)).astype(BF16).astype(F32)
        for k in range(2):
            for h in range(2):
                put(step0 + 3, 2 * k + h, lane_tile(back[128 * k:128 * k + 128], h))
        put(step0 + 3, 4, id_rows)
        exchange(step0 + 3)
        arrived(step0 + 3)
        tiles = cat(
            [cat([get(step0 + 3, 2 * k + h) for h in range(2)], 1) for k in range(2)], 0
        ).astype(BF16)
        far = interpolate(dot(in_pick, tiles).astype(BF16))

        @pl.when(which == 0)
        def _():
            pot = far + near_ref[...]
            pot_ref[...] = pot
            residual = (pot - target_ref[...]).astype(BF16)
            res_ref[...] = residual
            val[...] = residual.astype(F32)

        @pl.when(which == 1)
        def _():
            far_ref[...] = far

    for step in range(8):
        for row in range(5, 8):
            if step % 4 in (0, 3):
                put(step, row, jnp.zeros((NDEV, LANES), F32))
    val[...] = q_ref[...].astype(F32)
    load.wait()

    def both_passes(which, carry):
        evaluate(which * 4, which)
        return carry

    lax.fori_loop(0, 2, both_passes, 0)
    for step in range(8):
        sent(step)
    green_sent()


def far_kernel(q, near, target, stencil, green, dest, tile, tables):
    vmem = pl.BlockSpec(memory_space=pltpu.VMEM)
    hbm = pl.BlockSpec(memory_space=pl.ANY)
    return pl.pallas_call(
        kernel,
        out_shape=(
            jax.ShapeDtypeStruct((BLOCKS, LANES), F32),
            jax.ShapeDtypeStruct((BLOCKS, LANES), BF16),
            jax.ShapeDtypeStruct((BLOCKS, LANES), F32),
        ),
        in_specs=[vmem, vmem, vmem, hbm] + [vmem] * (3 + len(tables)),
        out_specs=(vmem, vmem, vmem),
        scratch_shapes=[
            pltpu.VMEM((BLOCKS * PANEL, CELLS), BF16),
            pltpu.VMEM((8, ROWS, LANES), F32),
            pltpu.VMEM((8, ROWS, LANES), F32),
            pltpu.VMEM((1024, LANES), F32),
            pltpu.VMEM((1024, LANES), F32),
            pltpu.VMEM((128, 512), F32),
            pltpu.VMEM((128, 512), F32),
            pltpu.VMEM((128, 128), F32),
            pltpu.VMEM((128, 256), F32),
            pltpu.VMEM((4, 256, 256), BF16),
            pltpu.VMEM((2, 256, 512), BF16),
            pltpu.VMEM((18, 256, 256), BF16),
            pltpu.SemaphoreType.DMA((8,)),
            pltpu.SemaphoreType.DMA((8,)),
            pltpu.SemaphoreType.DMA((32,)),
            pltpu.SemaphoreType.DMA,
            pltpu.SemaphoreType.DMA,
        ],
        compiler_params=pltpu.CompilerParams(collective_id=0, has_side_effects=True),
        name="far_field",
    )(q, near, target, stencil, green, dest, tile, *tables)


def extended_2(cells, sides, width):
    for axis, dim in sides:
        count = lax.axis_size(axis)
        ends = count - 1
        head = lax.slice_in_dim(cells, 0, width, axis=dim)
        tail = lax.slice_in_dim(cells, cells.shape[dim] - width, cells.shape[dim], axis=dim)
        cells = jnp.concatenate(
            [
                lax.ppermute(tail, axis, [(i, (i + 1) % count) for i in range(ends)]),
                cells,
                lax.ppermute(head, axis, [((i + 1) % count, i) for i in range(ends)]),
            ],
            axis=dim,
        )
    return cells


def local(tables, charges, target, stencil, near_matrix, green, block_dest, block_tile, near_offset):
    blocks = stencil.shape[0]
    block_size = stencil.shape[1]
    pair_count = near_offset.shape[1]
    couple = near_matrix.reshape(blocks, pair_count, block_size, block_size)
    positions = jnp.arange(blocks, dtype=jnp.int32)[:, None] + REACH + near_offset
    charge_blocks = charges.reshape(blocks, block_size)
    extended = extended_2(charge_blocks, ((("panel", "slab"), 0),), REACH)
    near = jnp.einsum(
        "bkps,bks->bp", couple, extended[positions], preferred_element_type=jnp.float32
    )
    twice = lambda x: jnp.concatenate([x, x], axis=1)
    pot, res, far = far_kernel(
        twice(charge_blocks), twice(near), twice(target.reshape(blocks, block_size)),
        stencil.reshape(blocks * block_size, stencil.shape[2]), green.T,
        block_dest.reshape(1, blocks), block_tile.reshape(1, blocks), tables,
    )
    potentials, residual = pot[:, :block_size], res[:, :block_size]
    terms = jnp.einsum("bkps,bp->bks", couple, residual, preferred_element_type=jnp.float32)
    extended = jnp.zeros((blocks + 2 * REACH, block_size), jnp.float32)
    extended = extended.at[positions.reshape(-1)].add(terms.reshape(-1, block_size))
    rims = jnp.concatenate([extended[:REACH], extended[blocks + REACH :]], axis=0)
    neighbour = extended_2(rims, ((("panel", "slab"), 0),), REACH)
    own_part = extended[REACH : blocks + REACH]
    own_part = own_part.at[:REACH].add(neighbour[:REACH])
    gradient = far[:, :block_size] + own_part.at[blocks - REACH :].add(neighbour[3 * REACH :])
    return (potentials.reshape(-1), gradient.reshape(-1))


def solution(mesh):
    made = make_tables()
    tables = [jnp.asarray(made[name]) for name in TABLES]
    return jax.shard_map(
        functools.partial(local, tables),
        mesh=mesh,
        in_specs=(
            P(("panel", "slab")),
            P(("panel", "slab")),
            P(("panel", "slab"), None, None),
            P(("panel", "slab"), None, None),
            P(None, ("panel", "slab")),
            P(("panel", "slab"), None),
            P(("panel", "slab")),
            P(("panel", "slab"), None),
        ),
        out_specs=(P(("panel", "slab")), P(("panel", "slab"))),
        check_vma=False,
    )
```

time: 353 us -> 168 us (0.48)
  the two profiles are of different devices: /device:TPU:1 before, /device:TPU:31 now
where the time goes in v1:
time: 168 us; the launch traced here: 167 us
  Pallas kernels  101 us (60%)
  local copies, waits for them, and re-layouts  26.6 us (16%)
  starting transfers between devices  16.4 us (10%)
  matrix products  10.2 us (6%)
  waiting for transfers between devices  7.2 us (4%)
  other arithmetic  4.46 us (3%)
    pallas_call x1, Pallas kernels, far_kernel(): pl.pallas_call(kernel, out_shape=(jax.ShapeDtypeStruct((BLOCKS, LANES), F...  101 us
    reshape x1, local copies, waits for them, and re-layouts, local(): couple = near_matrix.reshape(blocks, pair_count, block_size, block_size)  13 us
    ppermute x2, starting transfers between devices, extended_2(): lax.ppermute(tail, axis, [(i, (i + 1) % count) for i in range(ends)])  12.2 us
    unnamed x7, local copies, waits for them, and re-layouts  7.89 us
    ppermute x2, waiting for transfers between devices, extended_2(): lax.ppermute(head, axis, [((i + 1) % count, i) for i in range(ends)])  7.2 us
    dot_general x1, matrix products, local(): jnp.einsum('bkps,bks->bp', couple, extended[positions], preferred_element...  5.63 us
    dot_general x1, matrix products, local(): jnp.einsum('bkps,bp->bks', couple, residual, preferred_element_type=jnp.f...  4.61 us
    ppermute x2, starting transfers between devices, extended_2(): lax.ppermute(head, axis, [((i + 1) % count, i) for i in range(ends)])  4.27 us
  transfers between devices with their start and end apart: 4, of which 1 were waited for; matrix products, arithmetic and copies ran while one was open for 15% of the time, Pallas kernels for 0%

profile of v1, /device:TPU:31, one launch (start us, length us, event | category | flops | bytes accessed | tf_op | source)
XLA Modules:
  0.0 166.8 jit_solution(11951837479616828539)
XLA Ops:
  0.6 0.7 fusion.9
  1.3 0.1 slice.88
  1.4 2.4 %collective-permute-start.1 = (bf16[8,64]{1,0:T(8,128)(2,1)S(1)}, bf16[8,64]{1,0:T(8,128)(2,1)S(1)}, u32[]{:S(2)}, u32[]{:S(2)}) collective-permute-start(bf16[8,64]{1,0:T(8,128)(2,1)S(1)} %slice.88), channel_id=1, source_target_pairs={{1,0},{2,1},{3,2},{4,3},{5,4},{6,5},{7,6},{8,7},{9,8},{10,9},{11,1... | collective-permute-start | bytes 3080 | tf_op jit(solution)/shard_map/ppermute | solution.py:564
  3.8 0.1 slice.86
  3.9 7.4 %collective-permute-start = (bf16[8,64]{1,0:T(8,128)(2,1)S(1)}, bf16[8,64]{1,0:T(8,128)(2,1)S(1)}, u32[]{:S(2)}, u32[]{:S(2)}) collective-permute-start(bf16[8,64]{1,0:T(8,128)(2,1)S(1)} %slice.86), channel_id=1, source_target_pairs={{0,1},{1,2},{2,3},{3,4},{4,5},{5,6},{6,7},{7,8},{8,9},{9,10},{10,1... | collective-permute-start | bytes 3080 | tf_op jit(solution)/shard_map/ppermute | solution.py:562
  11.3 0.8 reshape.134
  12.1 0.7 pad_maximum_fusion.3.q_ref
  12.8 0.7 compare_select_fusion.1
  13.5 0.1 copy.19
  13.6 0.1 reshape.146
  13.7 0.1 copy.21
  13.8 0.1 reshape.141
  13.9 7.9 %copy.20 = bf16[128,4,4096]{0,2,1:T(8,128)(2,1)} copy(bf16[128,4,4096]{2,1,0:T(4,128)(2,1)} %param.24) | data formatting | bytes 8388608 | tf_op args[3]
  21.8 0.0 copy-start.2
  21.8 13.0 %copy.26 = bf16[128,4,64,64]{3,2,1,0:T(8,128)(2,1)} copy(bf16[128,4,64,64]{0,3,2,1:T(8,128)(2,1)} %bitcast.21) | data formatting | bytes 8388608 | tf_op jit(solution)/shard_map/reshape | solution.py:575
  34.9 0.0 copy-done.2
  34.9 0.1 reshape.136
  34.9 0.0 collective-permute-done.1
  34.9 0.0 collective-permute-done
  35.0 1.3 gather_fusion
  36.3 5.6 %fusion = f32[128,1,64,1]{2,1,3,0:T(1,128)S(1)} fusion(bf16[128,4,64,64]{3,2,1,0:T(8,128)(2,1)} %copy.26, bf16[128,4,64,1]{2,1,0,3:T(4,128)(2,1)S(1)} %bitcast.25), kind=kOutput, calls=%fused_computation.2 | convolution fusion | flops 4194304 | bytes 4292608 | tf_op jit(solution)/shard_map/bkps,bks->bp/dot_general | solution.py:579
  41.9 0.8 pad_maximum_fusion
  42.7 101.1 %far_field.1 = (f32[128,128]{1,0:T(8,128)}, bf16[128,128]{1,0:T(8,128)(2,1)}, f32[128,128]{1,0:T(8,128)}) custom-call(bf16[128,128]{1,0:T(8,128)(2,1)} %pad_maximum_fusion.3.q_ref, f32[128,128]{1,0:T(8,128)} %get-tuple-element.38.near_ref, f32[128,128]{1,0:T(8,128)} %get-tuple-element.39.target_ref, bf16[8192,256]{1,0:T(8,128)(2,1)} %bitcast.22, ...), custom_call_target="tpu_custom_call" | custom-call | tf_op jit(solution)/shard_map/far_field/pallas_call | solution.py:521
  143.8 0.8 slice_bitcast_fusion
  144.6 0.0 copy-start.1
  144.6 0.0 copy-start
  144.6 4.6 %fusion.2 = f32[128,1,4,64]{3,1,2,0:T(1,128)S(1)} fusion(bf16[128,4,64,64]{3,2,1,0:T(8,128)(2,1)} %copy.26, bf16[128,64,1,1]{1,0,2,3:T(8,128)(2,1)S(1)} %slice_bitcast_fusion), kind=kOutput, calls=%fused_computation.6 | convolution fusion | flops 4194304 | bytes 4341760 | tf_op jit(solution)/shard_map/bkps,bp->bks/dot_general | solution.py:589
  149.2 2.2 %scatter_custom_fusion = f32[144,64]{1,0:T(8,128)S(1)} fusion(s32[512]{0:T(512)S(1)} %bitcast.28, f32[512,64]{1,0:T(8,128)S(1)} %bitcast.23, f32[]{:T(128)} %constant.81.clone.1), kind=kCustom, calls=%fused_computation.10 | custom fusion | flops 32768 | bytes 36868 | tf_op jit(solution)/shard_map/scatter-add | solution.py:591
  151.5 4.8 %collective-permute-start.2 = (f32[8,64]{1,0:T(8,128)S(1)}, f32[8,64]{1,0:T(8,128)S(1)}, u32[]{:S(2)}, u32[]{:S(2)}) collective-permute-start(f32[8,64]{1,0:T(8,128)S(1)} %get-tuple-element.35), channel_id=1, source_target_pairs={{0,1},{1,2},{2,3},{3,4},{4,5},{5,6},{6,7},{7,8},{8,9},{9,10},{10,1... | collective-permute-start | bytes 6152 | tf_op jit(solution)/shard_map/ppermute | solution.py:562
  156.3 0.0 copy-done.1
  156.3 0.7 reshape.140
  157.0 1.9 %collective-permute-start.3 = (f32[8,64]{1,0:T(8,128)S(1)}, f32[8,64]{1,0:T(8,128)S(1)}, u32[]{:S(2)}, u32[]{:S(2)}) collective-permute-start(f32[8,64]{1,0:T(8,128)S(1)} %get-tuple-element.34), channel_id=1, source_target_pairs={{1,0},{2,1},{3,2},{4,3},{5,4},{6,5},{7,6},{8,7},{9,8},{10,9},{11,1... | collective-permute-start | bytes 6152 | tf_op jit(solution)/shard_map/ppermute | solution.py:564
  158.9 0.0 collective-permute-done.2
  158.9 7.2 %collective-permute-done.3 = f32[8,64]{1,0:T(8,128)S(1)} collective-permute-done((f32[8,64]{1,0:T(8,128)S(1)}, f32[8,64]{1,0:T(8,128)S(1)}, u32[]{:S(2)}, u32[]{:S(2)}) %collective-permute-start.3) | collective-permute-done | bytes 2080 | tf_op jit(solution)/shard_map/ppermute | solution.py:564
  166.1 0.0 copy-done
  166.1 0.7 reshape.143
  (9 shorter events, 0.1 us)
Async XLA Ops:
  1.4 33.5 %collective-permute-start.1 = (bf16[8,64]{1,0:T(8,128)(2,1)S(1)}, bf16[8,64]{1,0:T(8,128)(2,1)S(1)}, u32[]{:S(2)}, u32[]{:S(2)}) collective-permute-start(bf16[8,64]{1,0:T(8,128)(2,1)S(1)} %slice.88), channel_id=1, source_target_pairs={{1,0},{2,1},{3,2},{4,3},{5,4},{6,5},{7,6},{8,7},{9,8},{10,9},{11,1... | collective-permute-start | bytes 3080 | tf_op jit(solution)/shard_map/ppermute | solution.py:564
  3.9 31.1 %collective-permute-start = (bf16[8,64]{1,0:T(8,128)(2,1)S(1)}, bf16[8,64]{1,0:T(8,128)(2,1)S(1)}, u32[]{:S(2)}, u32[]{:S(2)}) collective-permute-start(bf16[8,64]{1,0:T(8,128)(2,1)S(1)} %slice.86), channel_id=1, source_target_pairs={{0,1},{1,2},{2,3},{3,4},{4,5},{5,6},{6,7},{7,8},{8,9},{9,10},{10,1... | collective-permute-start | bytes 3080 | tf_op jit(solution)/shard_map/ppermute | solution.py:562
  21.8 13.0 %copy-start.2 = (f32[8192]{0:T(1024)S(1)}, f32[8192]{0:T(1024)}, u32[]{:S(2)}) copy-start(f32[8192]{0:T(1024)} %param.22) | copy-start | bytes 98308
  144.6 11.7 %copy-start.1 = (f32[128,128]{1,0:T(8,128)S(1)}, f32[128,128]{1,0:T(8,128)}, u32[]{:S(2)}) copy-start(f32[128,128]{1,0:T(8,128)} %get-tuple-element.29) | copy-start | bytes 196612
  144.6 21.5 %copy-start = (f32[128,128]{1,0:T(8,128)S(1)}, f32[128,128]{1,0:T(8,128)}, u32[]{:S(2)}) copy-start(f32[128,128]{1,0:T(8,128)} %get-tuple-element.30) | copy-start | bytes 196612
  151.5 7.4 %collective-permute-start.2 = (f32[8,64]{1,0:T(8,128)S(1)}, f32[8,64]{1,0:T(8,128)S(1)}, u32[]{:S(2)}, u32[]{:S(2)}) collective-permute-start(f32[8,64]{1,0:T(8,128)S(1)} %get-tuple-element.35), channel_id=1, source_target_pairs={{0,1},{1,2},{2,3},{3,4},{4,5},{5,6},{6,7},{7,8},{8,9},{9,10},{10,1... | collective-permute-start | bytes 6152 | tf_op jit(solution)/shard_map/ppermute | solution.py:562
  157.0 9.1 %collective-permute-start.3 = (f32[8,64]{1,0:T(8,128)S(1)}, f32[8,64]{1,0:T(8,128)S(1)}, u32[]{:S(2)}, u32[]{:S(2)}) collective-permute-start(f32[8,64]{1,0:T(8,128)S(1)} %get-tuple-element.34), channel_id=1, source_target_pairs={{1,0},{2,1},{3,2},{4,3},{5,4},{6,5},{7,6},{8,7},{9,8},{10,9},{11,1... | collective-permute-start | bytes 6152 | tf_op jit(solution)/shard_map/ppermute | solution.py:564

commit v2 on v1

--- a/solution.py
+++ b/solution.py
@@ -99,12 +99,49 @@
     return jnp.concatenate(parts, axis=axis)
 
 
+COMBOS = sorted(
+    ((dz, dx) for dz in range(4) for dx in range(4)),
+    key=lambda c: -(min(c[0], 4 - c[0]) + min(c[1], 4 - c[1])),
+)
+Z_DIGITS = sum(c[0] << (2 * i) for i, c in enumerate(COMBOS))
+X_DIGITS = sum(c[1] << (2 * i) for i, c in enumerate(COMBOS))
+
+
+def encode(re, im):
+    top = jnp.abs(re[0])
+    for x in list(re[1:]) + list(im):
+        top = jnp.maximum(top, jnp.abs(x))
+    top = jnp.maximum(top, 2.0 ** -100)
+    power = jnp.floor(jnp.log2(top)) + 1.0
+    scale = jnp.exp2(14.0 - power)
+    code = power.astype(jnp.int32) + 128
+
+    def mantissa(x):
+        return jnp.minimum(x * scale + 16384.5, 32767.5).astype(jnp.int32)
+
+    return [
+        (((code >> (2 * j)) & 3) << 30) | (mantissa(re[j]) << 15) | mantissa(im[j])
+        for j in range(4)
+    ]
+
+
+def decode(words):
+    code = words[0] >> 30 & 3
+    for j in range(1, 4):
+        code = code | ((words[j] >> 30 & 3) << (2 * j))
+    scale = jnp.exp2(code.astype(F32) - 142.0)
+    re = [((w >> 15 & 32767).astype(F32) - 16384.0) * scale for w in words]
+    im = [((w & 32767).astype(F32) - 16384.0) * scale for w in words]
+    return re, im
+
+
 def kernel(
-    q_ref, near_ref, target_ref, stencil_hbm, green_ref, dest_ref, tile_ref,
+    q_ref, target_ref, stencil_hbm, near_hbm, green_ref, dest_ref, tile_ref, offset_ref,
     w1_ref, w2_ref, m0_ref, m0i_ref, a1_ref, w3_ref, t2_ref, t1_ref, tm_ref,
-    pot_ref, res_ref, far_ref,
-    stencil, sbuf, rbuf, gsend, grecv, ga, gb, val, tv, wf, wi, mats,
-    send_sem, recv_sem, gsend_sem, grecv_sem, load_sem,
+    pot_ref, grad_ref,
+    stencil, near_mat, sbuf, rbuf, swords, rwords, gsend, grecv, ga, gb, val, charge, goal, tv,
+    wf, wi, mats, xs, acc, near, ext, halo, rim,
+    send_sem, recv_sem, gsend_sem, grecv_sem, load_sem, near_sem, halo_sem, rim_sem,
 ):
     panel = lax.axis_index("panel")
     slab = lax.axis_index("slab")
@@ -114,25 +151,53 @@
     load = pltpu.make_async_copy(stencil_hbm, stencil, load_sem)
     load.start()
 
-    def peer_panel(i):
-        return ((pz + 2 + i // 8) % 4) * 8 + ((px + 2 + (i // 2) % 4) % 4) * 2 + (pc + i % 2) % 2
-
-    own = 20
+    def others(visit):
+        def body(g, carry):
+            z = (pz + ((Z_DIGITS >> (2 * g)) & 3)) % 4
+            x = (px + ((X_DIGITS >> (2 * g)) & 3)) % 4
+            for dy in (2, 1, 3, 0):
+                for dc in (1, 0):
+                    def go(z=z, x=x, dy=dy, dc=dc):
+                        visit(z * 8 + x * 2 + (pc + dc) % 2, (slab + dy) % 4)
+
+                    if dy == 0 and dc == 0:
+                        pl.when(g != 15)(go)
+                    else:
+                        go()
+            return carry
+
+        lax.fori_loop(0, 16, body, 0)
 
     barrier = pltpu.get_barrier_semaphore()
-
-    def greet(i, carry):
-        other = peer_panel(i)
-        for dy in (2, 3, 1):
-            pl.semaphore_signal(barrier, inc=1, device_id=(other, (slab + dy) % 4), device_id_type=MESH)
-
-        @pl.when(i != own)
-        def _():
-            pl.semaphore_signal(barrier, inc=1, device_id=(other, slab), device_id_type=MESH)
-
+    others(
+        lambda p, y: pl.semaphore_signal(barrier, inc=1, device_id=(p, y), device_id_type=MESH)
+    )
+
+    def near_load(b, carry):
+        pltpu.make_async_copy(
+            near_hbm.at[b], near_mat.at[pl.ds(pl.multiple_of(b * 4, 4), 4)], near_sem
+        ).start()
         return carry
 
-    lax.fori_loop(0, 32, greet, 0)
+    lax.fori_loop(0, BLOCKS, near_load, 0)
+
+    rows128, lanes128 = iota((128, 128), 0), iota((128, 128), 1)
+
+    def unfold(ref, out):
+        x = ref[...].astype(F32)
+        y = pltpu.roll(x, 64, 1)
+        low = iota((64, 128), 1) < 64
+        out[pl.ds(0, 64, stride=2), :] = jnp.where(low, x, y)
+        out[pl.ds(1, 64, stride=2), :] = jnp.where(low, y, x)
+
+    def fold(out, scr, value):
+        scr[...] = value
+        low = iota((64, 128), 1) < 64
+        out[...] = jnp.where(low, scr[pl.ds(0, 64, stride=2), :], scr[pl.ds(1, 64, stride=2), :])
+
+    unfold(q_ref, charge)
+    unfold(q_ref, val)
+    unfold(target_ref, goal)
 
     def pair(slot, value):
         hi, lo = split(value)
@@ -158,7 +223,6 @@
     pair(7, cat([cat([c, -s], 1), cat([s, c], 1)], 0))
     pair(8, cat([cat([c, s], 1), cat([-s, c], 1)], 0))
 
-    rows128, lanes128 = iota((128, 128), 0), iota((128, 128), 1)
     dest_row = dest_ref[...]
     tile_row = tile_ref[...]
 
@@ -180,49 +244,122 @@
     id_rows = jnp.where(lanes128 == 0, ids[:128], jnp.where(lanes128 == 1, ids[128:], 0.0))
     out_pick = out_pick.astype(BF16)
 
-    def exchange(step):
-        src, dst = sbuf.at[step], rbuf.at[step]
-        mine = pl.ds(pl.multiple_of(me * MSG, MSG), MSG)
-
-        def send(other, other_slab):
-            theirs = pl.ds(pl.multiple_of((other * SLABS + other_slab) * MSG, MSG), MSG)
+    def exchange(step, src, dst, stride, count):
+        mine = pl.ds(pl.multiple_of(me * stride, stride), count)
+
+        def send(p, y):
+            theirs = pl.ds(pl.multiple_of((p * SLABS + y) * stride, stride), count)
             pltpu.make_async_remote_copy(
                 src_ref=src.at[theirs],
                 dst_ref=dst.at[mine],
                 send_sem=send_sem.at[step],
                 recv_sem=recv_sem.at[step],
-                device_id=(other, other_slab),
+                device_id=(p, y),
                 device_id_type=MESH,
             ).start()
 
-        def body(i, carry):
-            other = peer_panel(i)
-            for dy in (2, 3, 1):
-                send(other, (slab + dy) % 4)
-
-            @pl.when(i != own)
-            def _():
-                send(other, slab)
-
+        others(send)
+        pltpu.make_async_copy(src.at[mine], dst.at[mine], recv_sem.at[step]).start()
+
+    def arrived(step, src, dst, count):
+        part = pl.ds(0, NDEV * count)
+        pltpu.make_async_copy(src.at[part], dst.at[part], recv_sem.at[step]).wait()
+
+    def sent(step, src, dst, count):
+        part = pl.ds(0, (NDEV - 1) * count)
+        pltpu.make_async_copy(src.at[part], dst.at[part], send_sem.at[step]).wait()
+
+    def put(slot, row, value):
+        sbuf[slot, pl.ds(row, NDEV, stride=MSG), :] = value
+
+    def get(slot, row):
+        return rbuf[slot, pl.ds(row, NDEV, stride=MSG), :]
+
+    def put_words(slot, re, im):
+        for j, w in enumerate(encode(re, im)):
+            swords[slot, pl.ds(j, NDEV, stride=4), :] = w
+
+    def get_words(slot):
+        return decode([rwords[slot, pl.ds(j, NDEV, stride=4), :] for j in range(4)])
+
+    def next_to(shift):
+        other = (me + shift + NDEV) % NDEV
+        return (other // SLABS, other % SLABS)
+
+    def edge_copies(src, rows_prev, rows_next, dst, sem):
+        for way, (shift, rows) in enumerate(((-1, rows_prev), (1, rows_next))):
+            yield pltpu.make_async_remote_copy(
+                src_ref=src.at[pl.ds(rows, REACH)],
+                dst_ref=dst.at[1 - way],
+                send_sem=sem.at[way],
+                recv_sem=sem.at[3 - way],
+                device_id=next_to(shift),
+                device_id_type=MESH,
+            )
+
+    halo_copies = list(edge_copies(charge, 0, BLOCKS - REACH, halo, halo_sem))
+    rim_copies = list(edge_copies(ext, BLOCKS, BLOCKS + REACH, rim, rim_sem))
+
+    def place(index):
+        return jnp.where(index < 128, index, jnp.where(index < 136, index - 136, index - 8))
+
+    def near_forward():
+        for copy in halo_copies:
+            copy.wait_recv()
+        before = jnp.where(me == 0, 0.0, halo[0])
+        after = jnp.where(me == NDEV - 1, 0.0, halo[1])
+        source = cat([charge[...], before, after], 0).astype(BF16)
+        spot = place(iota((128, 144), 1)) - iota((128, 144), 0)
+        for k in range(4):
+            pick = jnp.where(spot == column(offset_ref[k:k + 1, :]), one, zero).astype(BF16)
+            xs[pl.ds(k, 128, stride=4), :] = dot(pick, source)
+        pltpu.make_async_copy(near_mat, near_mat, near_sem).wait()
+        acc[...] = jnp.zeros((512, 128), F32)
+
+        def body(c, carry):
+            col = pl.ds(pl.multiple_of(c * 256, 256), 256)
+            gather = jnp.where(
+                iota((256, 128), 1) % 64 == c * 4 + iota((256, 128), 0) // 64, one, zero
+            ).astype(BF16)
+            for r in range(4):
+                row = pl.ds(128 * r, 128)
+                x = xs[row, :]
+                hi, lo = split(near_mat[row, col].astype(F32) * cat([x, x], 1))
+                acc[row, :] = acc[row, :] + (dot(hi, gather) + dot(lo, gather))
             return carry
 
-        lax.fori_loop(0, 32, body, 0)
-        pltpu.make_async_copy(src.at[mine], dst.at[mine], recv_sem.at[step]).start()
-
-    def arrived(step):
-        pltpu.make_async_copy(sbuf.at[step], rbuf.at[step], recv_sem.at[step]).wait()
-
-    def sent(step):
-        part = pl.ds(0, ROWS - MSG)
-        pltpu.make_async_copy(
-            sbuf.at[step, part], rbuf.at[step, part], send_sem.at[step]
-        ).wait()
-
-    def put(step, row, value):
-        sbuf[step, pl.ds(row, NDEV, stride=MSG), :] = value
-
-    def get(step, row):
-        return rbuf[step, pl.ds(row, NDEV, stride=MSG), :]
+        lax.fori_loop(0, 16, body, 0)
+        near[...] = sum(acc[pl.ds(k, 128, stride=4), :] for k in range(4))
+
+    def near_adjoint():
+        for k in range(4):
+            xs[pl.ds(k, 128, stride=4), :] = val[...]
+        acc[...] = jnp.zeros((512, 128), F32)
+
+        def body(c, carry):
+            col = pl.ds(pl.multiple_of(c * 256, 256), 256)
+            spread = jnp.where(
+                iota((128, 256), 0) == c * 4 + iota((128, 256), 1) // 64, one, zero
+            ).astype(BF16)
+            for r in range(4):
+                row = pl.ds(128 * r, 128)
+                p = near_mat[row, col].astype(F32) * dot(xs[row, :].astype(BF16), spread)
+                acc[row, :] = acc[row, :] + (p[:, :128] + p[:, 128:])
+            return carry
+
+        lax.fori_loop(0, 16, body, 0)
+
+    def near_scatter():
+        acc[...] = acc[...] + pltpu.roll(acc[...], 64, 1)
+        total = jnp.zeros((144, 128), F32)
+        spot = place(iota((144, 128), 0)) - iota((144, 128), 1)
+        for k in range(4):
+            pick = jnp.where(spot == offset_ref[k:k + 1, :], one, zero).astype(BF16)
+            hi, lo = split(acc[pl.ds(k, 128, stride=4), :])
+            total = total + (dot(pick, hi) + dot(pick, lo))
+        ext[...] = total
+        for copy in rim_copies:
+            copy.start()
 
     def pack(kk, carry):
         gsend[pl.ds(kk, 32, stride=32), :] = green_ref[:, pl.ds(pl.multiple_of(kk * LANES, LANES), LANES)]
@@ -355,28 +492,25 @@
             fixed.append(cat([jnp.where(h2, small[8 * j:8 * j + 8], out[:8]), out[8:]], 0))
         return fixed
 
-    def evaluate(step0, which):
+    def evaluate(which):
+        step0 = which * 4
+        first, last = which == 0, which == 1
+        fwd, inv_ = which * 2, which * 2 + 1
         out = project()
         for k in range(2):
             for h in range(2):
-                put(step0, 2 * k + h, lane_tile(out[128 * k:128 * k + 128], h))
-        put(step0, 4, id_rows)
-
-        @pl.when(which == 0)
+                put(fwd, 2 * k + h, lane_tile(out[128 * k:128 * k + 128], h))
+
+        @pl.when(first)
         def _():
+            put(0, 4, id_rows)
             pl.semaphore_wait(barrier, NDEV - 1)
-
-        exchange(step0)
-
-        @pl.when(which == 0)
-        def _():
+            exchange(0, sbuf.at[0], rbuf.at[0], MSG, 5)
             green_copies()
-
-        arrived(step0)
-
-        @pl.when(which == 0)
-        def _():
-            idm = get(step0, 4)
+            for copy in halo_copies:
+                copy.start()
+            arrived(0, sbuf.at[0], rbuf.at[0], 5)
+            idm = get(0, 4)
             tc = iota((128, 256), 1)
             for tr in range(2):
                 pick = cat(
@@ -390,8 +524,14 @@
                     wf[2 * tr + t] = dot_nt(mats[t], pick).astype(BF16)
                     wi[t, :, tr * 256:(tr + 1) * 256] = dot_nt(pick, mats[t]).astype(BF16)
 
+        @pl.when(last)
+        def _():
+            exchange(4, sbuf.at[2], rbuf.at[2], MSG, 4)
+            near_adjoint()
+            arrived(4, sbuf.at[2], rbuf.at[2], 4)
+
         tiles = split(
-            cat([cat([get(step0, 2 * k + h) for h in range(2)], 1) for k in range(2)], 0)
+            cat([cat([get(fwd, 2 * k + h) for h in range(2)], 1) for k in range(2)], 0)
         )
         c2, s2 = t2_ref[:, :LANES], t2_ref[:, LANES:]
         parts = []
@@ -402,24 +542,20 @@
                 parts.append(cat([re, im], 1))
         prod = dot3(split(cat(parts, 0)), mat(1))
         outs = special_rows(parts, 3, [prod[128 * j:128 * j + 128] for j in range(4)])
-        for j in range(4):
-            put(step0 + 1, j, outs[j][:, :LANES])
-            put(step0 + 1, 4 + j, outs[j][:, LANES:])
-        exchange(step0 + 1)
-
-        @pl.when(which == 0)
+        put_words(fwd, [o[:, :LANES] for o in outs], [o[:, LANES:] for o in outs])
+        exchange(step0 + 1, swords.at[fwd], rwords.at[fwd], 4, 4)
+
+        @pl.when(first)
         def _():
             green_ready()
 
-        arrived(step0 + 1)
-        x = cat(
-            [
-                cat([get(step0 + 1, j) for j in range(4)], 1),
-                cat([get(step0 + 1, 4 + j) for j in range(4)], 1),
-            ],
-            0,
-        )
-        y = dot3(mat(5), split(x))
+        @pl.when(last)
+        def _():
+            near_scatter()
+
+        arrived(step0 + 1, swords.at[fwd], rwords.at[fwd], 4)
+        re, im = get_words(fwd)
+        y = dot3(mat(5), split(cat([cat(re, 1), cat(im, 1)], 0)))
         re, im = cmul(y[:128], y[128:], t1_ref[:, :512], t1_ref[:, 512:])
         r = [lane_tile(re, j) for j in range(4)]
         i = [lane_tile(im, j) for j in range(4)]
@@ -458,12 +594,16 @@
         inv = mat(6)
         yr = dot3((inv[0][:128], inv[1][:128]), stacked[0])
         yi = dot3((inv[0][128:], inv[1][128:]), stacked[1])
-        for j in range(4):
-            put(step0 + 2, j, lane_tile(yr, j))
-            put(step0 + 2, 4 + j, lane_tile(yi, j))
-        exchange(step0 + 2)
-        arrived(step0 + 2)
-        parts = [cat([get(step0 + 2, j), get(step0 + 2, 4 + j)], 1) for j in range(4)]
+        put_words(inv_, [lane_tile(yr, j) for j in range(4)], [lane_tile(yi, j) for j in range(4)])
+        exchange(step0 + 2, swords.at[inv_], rwords.at[inv_], 4, 4)
+
+        @pl.when(first)
+        def _():
+            near_forward()
+
+        arrived(step0 + 2, swords.at[inv_], rwords.at[inv_], 4)
+        re, im = get_words(inv_)
+        parts = [cat([re[j], im[j]], 1) for j in range(4)]
         prod = dot3(split(cat(parts, 0)), mat(2))
         outs = special_rows(parts, 4, [prod[128 * j:128 * j + 128] for j in range(4)])
         zs = [cmul_conj(o[:, :LANES], o[:, LANES:], c2, s2) for o in outs]
@@ -477,124 +617,99 @@
         back = dot3((wi[0], wi[1]), split(y)).astype(BF16).astype(F32)
         for k in range(2):
             for h in range(2):
-                put(step0 + 3, 2 * k + h, lane_tile(back[128 * k:128 * k + 128], h))
-        put(step0 + 3, 4, id_rows)
-        exchange(step0 + 3)
-        arrived(step0 + 3)
+                put(inv_, 2 * k + h, lane_tile(back[128 * k:128 * k + 128], h))
+        exchange(step0 + 3, sbuf.at[inv_], rbuf.at[inv_], MSG, 4)
+        arrived(step0 + 3, sbuf.at[inv_], rbuf.at[inv_], 4)
         tiles = cat(
-            [cat([get(step0 + 3, 2 * k + h) for h in range(2)], 1) for k in range(2)], 0
+            [cat([get(inv_, 2 * k + h) for h in range(2)], 1) for k in range(2)], 0
         ).astype(BF16)
         far = interpolate(dot(in_pick, tiles).astype(BF16))
 
-        @pl.when(which == 0)
+        @pl.when(first)
         def _():
-            pot = far + near_ref[...]
-            pot_ref[...] = pot
-            residual = (pot - target_ref[...]).astype(BF16)
-            res_ref[...] = residual
-            val[...] = residual.astype(F32)
-
-        @pl.when(which == 1)
+            pot = far + near[...]
+            val[...] = (pot - goal[...]).astype(BF16).astype(F32)
+            fold(pot_ref, tv2, pot)
+
+        @pl.when(last)
         def _():
-            far_ref[...] = far
-
-    for step in range(8):
-        for row in range(5, 8):
-            if step % 4 in (0, 3):
-                put(step, row, jnp.zeros((NDEV, LANES), F32))
-    val[...] = q_ref[...].astype(F32)
+            for copy in rim_copies:
+                copy.wait_recv()
+            before = jnp.where(me == 0, 0.0, rim[0])
+            after = jnp.where(me == NDEV - 1, 0.0, rim[1])
+            grad = far + ext[:BLOCKS, :]
+            grad = cat(
+                [grad[:REACH] + before, grad[REACH:BLOCKS - REACH], grad[BLOCKS - REACH:] + after], 0
+            )
+            fold(grad_ref, tv2, grad)
+
+    tv2 = goal
     load.wait()
 
     def both_passes(which, carry):
-        evaluate(which * 4, which)
+        evaluate(which)
         return carry
 
     lax.fori_loop(0, 2, both_passes, 0)
-    for step in range(8):
-        sent(step)
+    for p in range(2):
+        sent(4 * p, sbuf.at[2 * p], rbuf.at[2 * p], 5 - p)
+        sent(4 * p + 1, swords.at[2 * p], rwords.at[2 * p], 4)
+        sent(4 * p + 2, swords.at[2 * p + 1], rwords.at[2 * p + 1], 4)
+        sent(4 * p + 3, sbuf.at[2 * p + 1], rbuf.at[2 * p + 1], 4)
     green_sent()
-
-
-def far_kernel(q, near, target, stencil, green, dest, tile, tables):
+    for copy in halo_copies + rim_copies:
+        copy.wait_send()
+
+
+def local(tables, charges, target, stencil, near_matrix, green, block_dest, block_tile, near_offset):
     vmem = pl.BlockSpec(memory_space=pltpu.VMEM)
     hbm = pl.BlockSpec(memory_space=pl.ANY)
-    return pl.pallas_call(
+    pot, grad = pl.pallas_call(
         kernel,
-        out_shape=(
-            jax.ShapeDtypeStruct((BLOCKS, LANES), F32),
-            jax.ShapeDtypeStruct((BLOCKS, LANES), BF16),
-            jax.ShapeDtypeStruct((BLOCKS, LANES), F32),
-        ),
-        in_specs=[vmem, vmem, vmem, hbm] + [vmem] * (3 + len(tables)),
-        out_specs=(vmem, vmem, vmem),
+        out_shape=(jax.ShapeDtypeStruct((64, LANES), F32),) * 2,
+        in_specs=[vmem, vmem, hbm, hbm] + [vmem] * (4 + len(tables)),
+        out_specs=(vmem, vmem),
         scratch_shapes=[
             pltpu.VMEM((BLOCKS * PANEL, CELLS), BF16),
-            pltpu.VMEM((8, ROWS, LANES), F32),
-            pltpu.VMEM((8, ROWS, LANES), F32),
+            pltpu.VMEM((4 * BLOCKS, PANEL * PANEL), BF16),
+            pltpu.VMEM((4, ROWS, LANES), F32),
+            pltpu.VMEM((4, ROWS, LANES), F32),
+            pltpu.VMEM((4, 4 * NDEV, LANES), jnp.int32),
+            pltpu.VMEM((4, 4 * NDEV, LANES), jnp.int32),
             pltpu.VMEM((1024, LANES), F32),
             pltpu.VMEM((1024, LANES), F32),
             pltpu.VMEM((128, 512), F32),
             pltpu.VMEM((128, 512), F32),
             pltpu.VMEM((128, 128), F32),
+            pltpu.VMEM((128, 128), F32),
+            pltpu.VMEM((128, 128), F32),
             pltpu.VMEM((128, 256), F32),
             pltpu.VMEM((4, 256, 256), BF16),
             pltpu.VMEM((2, 256, 512), BF16),
             pltpu.VMEM((18, 256, 256), BF16),
+            pltpu.VMEM((512, LANES), F32),
+            pltpu.VMEM((512, LANES), F32),
+            pltpu.VMEM((128, LANES), F32),
+            pltpu.VMEM((144, LANES), F32),
+            pltpu.VMEM((2, REACH, LANES), F32),
+            pltpu.VMEM((2, REACH, LANES), F32),
             pltpu.SemaphoreType.DMA((8,)),
             pltpu.SemaphoreType.DMA((8,)),
             pltpu.SemaphoreType.DMA((32,)),
             pltpu.SemaphoreType.DMA,
             pltpu.SemaphoreType.DMA,
+            pltpu.SemaphoreType.DMA,
+            pltpu.SemaphoreType.DMA((4,)),
+            pltpu.SemaphoreType.DMA((4,)),
         ],
         compiler_params=pltpu.CompilerParams(collective_id=0, has_side_effects=True),
-        name="far_field",
-    )(q, near, target, stencil, green, dest, tile, *tables)
-
-
-def extended_2(cells, sides, width):
-    for axis, dim in sides:
-        count = lax.axis_size(axis)
-        ends = count - 1
-        head = lax.slice_in_dim(cells, 0, width, axis=dim)
-        tail = lax.slice_in_dim(cells, cells.shape[dim] - width, cells.shape[dim], axis=dim)
-        cells = jnp.concatenate(
-            [
-                lax.ppermute(tail, axis, [(i, (i + 1) % count) for i in range(ends)]),
-                cells,
-                lax.ppermute(head, axis, [((i + 1) % count, i) for i in range(ends)]),
-            ],
-            axis=dim,
-        )
-    return cells
-
-
-def local(tables, charges, target, stencil, near_matrix, green, block_dest, block_tile, near_offset):
-    blocks = stencil.shape[0]
-    block_size = stencil.shape[1]
-    pair_count = near_offset.shape[1]
-    couple = near_matrix.reshape(blocks, pair_count, block_size, block_size)
-    positions = jnp.arange(blocks, dtype=jnp.int32)[:, None] + REACH + near_offset
-    charge_blocks = charges.reshape(blocks, block_size)
-    extended = extended_2(charge_blocks, ((("panel", "slab"), 0),), REACH)
-    near = jnp.einsum(
-        "bkps,bks->bp", couple, extended[positions], preferred_element_type=jnp.float32
+        name="panel_solver",
+    )(
+        charges.reshape(64, LANES), target.reshape(64, LANES),
+        stencil.reshape(BLOCKS * PANEL, CELLS), near_matrix, green.T,
+        block_dest.reshape(1, BLOCKS), block_tile.reshape(1, BLOCKS), near_offset.T, *tables,
     )
-    twice = lambda x: jnp.concatenate([x, x], axis=1)
-    pot, res, far = far_kernel(
-        twice(charge_blocks), twice(near), twice(target.reshape(blocks, block_size)),
-        stencil.reshape(blocks * block_size, stencil.shape[2]), green.T,
-        block_dest.reshape(1, blocks), block_tile.reshape(1, blocks), tables,
-    )
-    potentials, residual = pot[:, :block_size], res[:, :block_size]
-    terms = jnp.einsum("bkps,bp->bks", couple, residual, preferred_element_type=jnp.float32)
-    extended = jnp.zeros((blocks + 2 * REACH, block_size), jnp.float32)
-    extended = extended.at[positions.reshape(-1)].add(terms.reshape(-1, block_size))
-    rims = jnp.concatenate([extended[:REACH], extended[blocks + REACH :]], axis=0)
-    neighbour = extended_2(rims, ((("panel", "slab"), 0),), REACH)
-    own_part = extended[REACH : blocks + REACH]
-    own_part = own_part.at[:REACH].add(neighbour[:REACH])
-    gradient = far[:, :block_size] + own_part.at[blocks - REACH :].add(neighbour[3 * REACH :])
-    return (potentials.reshape(-1), gradient.reshape(-1))
+    return (pot.reshape(-1), grad.reshape(-1))
 
 
 def solution(mesh):

time: 168 us -> 88.5 us (0.53)
  the two profiles are of different devices: /device:TPU:31 before, /device:TPU:1 now
where the time goes in v2:
time: 88.5 us; the launch traced here: 88.2 us
  Pallas kernels  84.8 us (96%)
  local copies, waits for them, and re-layouts  2.75 us (3%)
    pallas_call x1, Pallas kernels, local(): pl.pallas_call(kernel, out_shape=(jax.ShapeDtypeStruct((64, LANES), F32),...  84.8 us
    unnamed x2, local copies, waits for them, and re-layouts  2.75 us

profile of v2, /device:TPU:1, one launch (start us, length us, event | category | flops | bytes accessed | tf_op | source)
XLA Modules:
  0.0 88.2 jit_solution(344788227340099628)
XLA Ops:
  0.6 84.8 %panel_solver.1 = (f32[64,128]{1,0:T(8,128)}, f32[64,128]{1,0:T(8,128)}) custom-call(bf16[64,128]{1,0:T(8,128)(2,1)} %bitcast.14, f32[64,128]{1,0:T(8,128)} %bitcast.11, bf16[8192,256]{1,0:T(8,128)(2,1)} %bitcast.9, bf16[128,4,4096]{2,1,0:T(4,128)(2,1)} %near_hbm.1, f32[32,4096]{1,0:T(8,128)} %bitcast.10, s32[1,128]{1,0:T(1,128)} %bitcast.16, ...), custom_call_target="tpu_custom_call" | custom-call | tf_op jit(solution)/shard_map/panel_solver/pallas_call | solution.py:667
  85.5 1.4 %copy.21 = f32[8192]{0:T(1024)} copy(f32[8192]{0:T(1024)} %bitcast.13) | data formatting | bytes 65536
  86.8 1.4 %copy.22 = f32[8192]{0:T(1024)} copy(f32[8192]{0:T(1024)} %bitcast.12) | data formatting | bytes 65536

commit v3 on v2

--- a/solution.py
+++ b/solution.py
@@ -23,7 +23,10 @@
 MESH = pl.DeviceIdType.MESH
 F32 = jnp.float32
 BF16 = jnp.bfloat16
-TABLES = ("w1", "w2", "m0", "m0i", "a1", "w3", "t2", "t1", "tm")
+TABLES = (("w1", 256), ("m0", 256), ("m0i", 256), ("w2", 128), ("a1", 128), ("w3", 128), ("t2", 128),
+          ("c0", 128), ("c1", 128), ("s0", 128), ("s1", 128), ("tm", 8))
+START = {name: sum(n for _, n in TABLES[:i]) for i, (name, _) in enumerate(TABLES)}
+TABLE_ROWS = sum(n for _, n in TABLES)
 
 
 def make_tables():
@@ -66,12 +69,13 @@
     th[0] = 0.0
     out["t2"] = np.concatenate([np.cos(th), np.sin(th)], 1)
     th = np.repeat(angle(np.arange(128), np.arange(32), GRID), 16, axis=1)
-    out["t1"] = np.concatenate([np.cos(th), np.sin(th)], 1)
+    out["c0"], out["c1"] = np.cos(th[:, :256]), np.cos(th[:, 256:])
+    out["s0"], out["s1"] = np.sin(th[:, :256]), np.sin(th[:, 256:])
     th = np.repeat(angle(np.arange(4), np.arange(8), 32), 16, axis=1)
     tm = np.zeros((8, 256))
     tm[:4] = np.concatenate([np.cos(th), np.sin(th)], 1)
     out["tm"] = tm
-    return {k: np.asarray(v, np.float32) for k, v in out.items()}
+    return np.concatenate([out[name] for name, _ in TABLES], 0).astype(np.float32)
 
 
 def dot(a, b):
@@ -136,10 +140,10 @@
 
 
 def kernel(
-    q_ref, target_ref, stencil_hbm, near_hbm, green_ref, dest_ref, tile_ref, offset_ref,
-    w1_ref, w2_ref, m0_ref, m0i_ref, a1_ref, w3_ref, t2_ref, t1_ref, tm_ref,
-    pot_ref, grad_ref,
-    stencil, near_mat, sbuf, rbuf, swords, rwords, gsend, grecv, ga, gb, val, charge, goal, tv,
+    q_hbm, target_hbm, stencil_hbm, near_hbm, green_hbm, dest_hbm, tile_hbm, offset_hbm, table_hbm,
+    out_ref,
+    q_ref, target_ref, green_ref, dest_ref, tile_ref, offset_ref, table,
+    stencil, near_mat, sbuf, rbuf, sback, rback, swords, rwords, gsend, grecv, ga, gb, val, charge, goal, tv,
     wf, wi, mats, xs, acc, near, ext, halo, rim,
     send_sem, recv_sem, gsend_sem, grecv_sem, load_sem, near_sem, halo_sem, rim_sem,
 ):
@@ -148,8 +152,23 @@
     me = panel * SLABS + slab
     pz, px, pc = panel // 8, (panel // 2) % 4, panel % 2
 
-    load = pltpu.make_async_copy(stencil_hbm, stencil, load_sem)
-    load.start()
+    loads = {}
+    for i, (name, src, dst) in enumerate((
+        ("q", q_hbm, q_ref), ("dest", dest_hbm, dest_ref), ("tile", tile_hbm, tile_ref),
+        ("stencil", stencil_hbm, stencil), ("table", table_hbm, table),
+        ("green", green_hbm, green_ref), ("offset", offset_hbm, offset_ref),
+        ("target", target_hbm, target_ref),
+    )):
+        loads[name] = pltpu.make_async_copy(src, dst, load_sem.at[i])
+        loads[name].start()
+
+    def rows_at(name):
+        n = dict(TABLES)[name]
+        return table[START[name]:START[name] + n, :]
+
+    def half_at(name, half):
+        n = dict(TABLES)[name]
+        return table[START[name]:START[name] + n, half * LANES:(half + 1) * LANES]
 
     def others(visit):
         def body(g, carry):
@@ -179,8 +198,6 @@
         ).start()
         return carry
 
-    lax.fori_loop(0, BLOCKS, near_load, 0)
-
     rows128, lanes128 = iota((128, 128), 0), iota((128, 128), 1)
 
     def unfold(ref, out):
@@ -190,14 +207,16 @@
         out[pl.ds(0, 64, stride=2), :] = jnp.where(low, x, y)
         out[pl.ds(1, 64, stride=2), :] = jnp.where(low, y, x)
 
-    def fold(out, scr, value):
-        scr[...] = value
+    def fold(row, value):
+        goal[...] = value
         low = iota((64, 128), 1) < 64
-        out[...] = jnp.where(low, scr[pl.ds(0, 64, stride=2), :], scr[pl.ds(1, 64, stride=2), :])
-
+        out_ref[row:row + 64, :] = jnp.where(
+            low, goal[pl.ds(0, 64, stride=2), :], goal[pl.ds(1, 64, stride=2), :]
+        )
+
+    loads["q"].wait()
     unfold(q_ref, charge)
-    unfold(q_ref, val)
-    unfold(target_ref, goal)
+    val[...] = charge[...]
 
     def pair(slot, value):
         hi, lo = split(value)
@@ -207,22 +226,25 @@
     def mat(slot):
         return mats[2 * slot], mats[2 * slot + 1]
 
-    def circle(ref):
-        return ref[:, :LANES], ref[:, LANES:]
-
-    pair(0, w1_ref[...])
-    c, s = circle(w2_ref)
-    pair(1, cat([cat([c, -s], 1), cat([s, c], 1)], 0))
-    pair(2, cat([cat([c, s], 1), cat([-s, c], 1)], 0))
-    pair(3, m0_ref[...])
-    pair(4, m0i_ref[...])
-    c, s = circle(a1_ref)
-    pair(5, cat([cat([c, s], 1), cat([-s, c], 1)], 0))
-    pair(6, cat([cat([c, -s], 1), cat([s, c], 1)], 0))
-    c, s = circle(w3_ref)
-    pair(7, cat([cat([c, -s], 1), cat([s, c], 1)], 0))
-    pair(8, cat([cat([c, s], 1), cat([-s, c], 1)], 0))
-
+    def split_tables():
+        def circle(name):
+            return half_at(name, 0), half_at(name, 1)
+
+        pair(0, rows_at("w1"))
+        c, s = circle("w2")
+        pair(1, cat([cat([c, -s], 1), cat([s, c], 1)], 0))
+        pair(2, cat([cat([c, s], 1), cat([-s, c], 1)], 0))
+        pair(3, rows_at("m0"))
+        pair(4, rows_at("m0i"))
+        c, s = circle("a1")
+        pair(5, cat([cat([c, s], 1), cat([-s, c], 1)], 0))
+        pair(6, cat([cat([c, -s], 1), cat([s, c], 1)], 0))
+        c, s = circle("w3")
+        pair(7, cat([cat([c, -s], 1), cat([s, c], 1)], 0))
+        pair(8, cat([cat([c, s], 1), cat([-s, c], 1)], 0))
+
+    loads["dest"].wait()
+    loads["tile"].wait()
     dest_row = dest_ref[...]
     tile_row = tile_ref[...]
 
@@ -237,9 +259,8 @@
     out_pick = cat(
         [jnp.where((dest_row == rows128) & (rank_row == k), one, zero) for k in range(2)], 0
     )
-    in_pick = cat(
-        [jnp.where((dest_col == lanes128) & (rank_col == k), one, zero) for k in range(2)], 1
-    ).astype(BF16)
+    wanted = iota((128, 512), 1) - 4 * dest_col - 2 * rank_col
+    in_pick = [jnp.where(wanted == h, one, zero).astype(BF16) for h in range(2)]
     ids = jnp.sum(out_pick * (tile_row + 1).astype(F32), axis=1, keepdims=True)
     id_rows = jnp.where(lanes128 == 0, ids[:128], jnp.where(lanes128 == 1, ids[128:], 0.0))
     out_pick = out_pick.astype(BF16)
@@ -304,6 +325,7 @@
         return jnp.where(index < 128, index, jnp.where(index < 136, index - 136, index - 8))
 
     def near_forward():
+        loads["offset"].wait()
         for copy in halo_copies:
             copy.wait_recv()
         before = jnp.where(me == 0, 0.0, halo[0])
@@ -364,8 +386,6 @@
     def pack(kk, carry):
         gsend[pl.ds(kk, 32, stride=32), :] = green_ref[:, pl.ds(pl.multiple_of(kk * LANES, LANES), LANES)]
         return carry
-
-    lax.fori_loop(0, 32, pack, 0)
 
     def green_copies():
         k2 = me // 8
@@ -499,19 +519,29 @@
         out = project()
         for k in range(2):
             for h in range(2):
-                put(fwd, 2 * k + h, lane_tile(out[128 * k:128 * k + 128], h))
+                put(which, 2 * k + h, lane_tile(out[128 * k:128 * k + 128], h))
 
         @pl.when(first)
         def _():
             put(0, 4, id_rows)
             pl.semaphore_wait(barrier, NDEV - 1)
             exchange(0, sbuf.at[0], rbuf.at[0], MSG, 5)
-            green_copies()
             for copy in halo_copies:
                 copy.start()
+            loads["green"].wait()
+            lax.fori_loop(0, 32, pack, 0)
+            green_copies()
+            lax.fori_loop(0, BLOCKS, near_load, 0)
+            loads["table"].wait()
+            split_tables()
+            loads["target"].wait()
+            unfold(target_ref, goal)
             arrived(0, sbuf.at[0], rbuf.at[0], 5)
             idm = get(0, 4)
             tc = iota((128, 256), 1)
+            for k in range(2):
+                xs[pl.ds(k, 128, stride=2), :] = jnp.broadcast_to(idm[:, k:k + 1], (128, 128))
+            ordered = xs[:256, :1].astype(jnp.int32)
             for tr in range(2):
                 pick = cat(
                     [
@@ -520,20 +550,25 @@
                     ],
                     0,
                 ).astype(BF16)
+                back_pick = jnp.where(
+                    ordered == iota((256, 256), 1) + (tr * 256 + 1), one, zero
+                ).astype(BF16)
                 for t in range(2):
                     wf[2 * tr + t] = dot_nt(mats[t], pick).astype(BF16)
-                    wi[t, :, tr * 256:(tr + 1) * 256] = dot_nt(pick, mats[t]).astype(BF16)
+                    wi[t, :, tr * 256:(tr + 1) * 256] = dot_nt(back_pick, mats[t]).astype(BF16)
 
         @pl.when(last)
         def _():
-            exchange(4, sbuf.at[2], rbuf.at[2], MSG, 4)
+            exchange(4, sbuf.at[1], rbuf.at[1], MSG, 4)
             near_adjoint()
-            arrived(4, sbuf.at[2], rbuf.at[2], 4)
+            arrived(4, sbuf.at[1], rbuf.at[1], 4)
 
         tiles = split(
-            cat([cat([get(fwd, 2 * k + h) for h in range(2)], 1) for k in range(2)], 0)
+            cat([cat([get(which, 2 * k + h) for h in range(2)], 1) for k in range(2)], 0)
         )
-        c2, s2 = t2_ref[:, :LANES], t2_ref[:, LANES:]
+        c2, s2 = half_at("t2", 0), half_at("t2", 1)
+        c1 = cat([rows_at("c0"), rows_at("c1")], 1)
+        s1 = cat([rows_at("s0"), rows_at("s1")], 1)
         parts = []
         for tr in range(2):
             y = dot3((wf[2 * tr], wf[2 * tr + 1]), tiles)
@@ -556,7 +591,7 @@
         arrived(step0 + 1, swords.at[fwd], rwords.at[fwd], 4)
         re, im = get_words(fwd)
         y = dot3(mat(5), split(cat([cat(re, 1), cat(im, 1)], 0)))
-        re, im = cmul(y[:128], y[128:], t1_ref[:, :512], t1_ref[:, 512:])
+        re, im = cmul(y[:128], y[128:], c1, s1)
         r = [lane_tile(re, j) for j in range(4)]
         i = [lane_tile(im, j) for j in range(4)]
         er, ei, dr, di = r[0] + r[2], i[0] + i[2], r[0] - r[2], i[0] - i[2]
@@ -564,7 +599,7 @@
         vs = [(er + fr, ei + fi), (dr + hi_, di - hr), (er - fr, ei - fi), (dr - hi_, di + hr)]
         parts = []
         for m in range(4):
-            cm, sm = tm_ref[m:m + 1, :LANES], tm_ref[m:m + 1, LANES:]
+            cm, sm = half_at("tm", 0)[m:m + 1], half_at("tm", 1)[m:m + 1]
             parts.append(cat(list(cmul(vs[m][0], vs[m][1], cm, sm)), 1))
         f = dot3(split(cat(parts, 0)), mat(7))
         both = []
@@ -578,7 +613,7 @@
         for e in range(2):
             vs = []
             for m in range(4):
-                cm, sm = tm_ref[m:m + 1, :LANES], tm_ref[m:m + 1, LANES:]
+                cm, sm = half_at("tm", 0)[m:m + 1], half_at("tm", 1)[m:m + 1]
                 pm = p[512 * e + 128 * m:512 * e + 128 * m + 128]
                 vs.append(cmul_conj(pm[:, :LANES], pm[:, LANES:], cm, sm))
             r = [v[0] for v in vs]
@@ -587,8 +622,7 @@
             fr, fi, hr, hi_ = r[1] + r[3], i[1] + i[3], r[1] - r[3], i[1] - i[3]
             zs = [(er + fr, ei + fi), (dr - hi_, di + hr), (er - fr, ei - fi), (dr + hi_, di - hr)]
             re, im = cmul_conj(
-                cat([z[0] for z in zs], 1), cat([z[1] for z in zs], 1),
-                t1_ref[:, :512], t1_ref[:, 512:],
+                cat([z[0] for z in zs], 1), cat([z[1] for z in zs], 1), c1, s1,
             )
             stacked.append(split(cat([re, im], 0)))
         inv = mat(6)
@@ -614,22 +648,20 @@
             ],
             0,
         )
-        back = dot3((wi[0], wi[1]), split(y)).astype(BF16).astype(F32)
-        for k in range(2):
-            for h in range(2):
-                put(inv_, 2 * k + h, lane_tile(back[128 * k:128 * k + 128], h))
-        exchange(step0 + 3, sbuf.at[inv_], rbuf.at[inv_], MSG, 4)
-        arrived(step0 + 3, sbuf.at[inv_], rbuf.at[inv_], 4)
-        tiles = cat(
-            [cat([get(inv_, 2 * k + h) for h in range(2)], 1) for k in range(2)], 0
-        ).astype(BF16)
-        far = interpolate(dot(in_pick, tiles).astype(BF16))
+        back = dot3((wi[0], wi[1]), split(y))
+        for h in range(2):
+            xs[pl.ds(h, 256, stride=2), :] = lane_tile(back, h)
+        sback[which] = xs[...].astype(BF16)
+        exchange(step0 + 3, sback.at[which], rback.at[which], 4, 4)
+        arrived(step0 + 3, sback.at[which], rback.at[which], 4)
+        tiles = rback[which]
+        far = interpolate(cat([dot(in_pick[h], tiles) for h in range(2)], 1).astype(BF16))
 
         @pl.when(first)
         def _():
             pot = far + near[...]
             val[...] = (pot - goal[...]).astype(BF16).astype(F32)
-            fold(pot_ref, tv2, pot)
+            fold(0, pot)
 
         @pl.when(last)
         def _():
@@ -641,10 +673,9 @@
             grad = cat(
                 [grad[:REACH] + before, grad[REACH:BLOCKS - REACH], grad[BLOCKS - REACH:] + after], 0
             )
-            fold(grad_ref, tv2, grad)
-
-    tv2 = goal
-    load.wait()
+            fold(64, grad)
+
+    loads["stencil"].wait()
 
     def both_passes(which, carry):
         evaluate(which)
@@ -652,28 +683,35 @@
 
     lax.fori_loop(0, 2, both_passes, 0)
     for p in range(2):
-        sent(4 * p, sbuf.at[2 * p], rbuf.at[2 * p], 5 - p)
+        sent(4 * p, sbuf.at[p], rbuf.at[p], 5 - p)
         sent(4 * p + 1, swords.at[2 * p], rwords.at[2 * p], 4)
         sent(4 * p + 2, swords.at[2 * p + 1], rwords.at[2 * p + 1], 4)
-        sent(4 * p + 3, sbuf.at[2 * p + 1], rbuf.at[2 * p + 1], 4)
+        sent(4 * p + 3, sback.at[p], rback.at[p], 4)
     green_sent()
     for copy in halo_copies + rim_copies:
         copy.wait_send()
 
 
-def local(tables, charges, target, stencil, near_matrix, green, block_dest, block_tile, near_offset):
-    vmem = pl.BlockSpec(memory_space=pltpu.VMEM)
-    hbm = pl.BlockSpec(memory_space=pl.ANY)
-    pot, grad = pl.pallas_call(
+def local(table, charges, target, stencil, near_matrix, green, block_dest, block_tile, near_offset):
+    out = pl.pallas_call(
         kernel,
-        out_shape=(jax.ShapeDtypeStruct((64, LANES), F32),) * 2,
-        in_specs=[vmem, vmem, hbm, hbm] + [vmem] * (4 + len(tables)),
-        out_specs=(vmem, vmem),
+        out_shape=jax.ShapeDtypeStruct((128, LANES), F32),
+        in_specs=[pl.BlockSpec(memory_space=pl.ANY)] * 9,
+        out_specs=pl.BlockSpec(memory_space=pltpu.VMEM),
         scratch_shapes=[
+            pltpu.VMEM((64, LANES), BF16),
+            pltpu.VMEM((64, LANES), F32),
+            pltpu.VMEM((32, GRID), F32),
+            pltpu.VMEM((1, LANES), jnp.int32),
+            pltpu.VMEM((1, LANES), jnp.int32),
+            pltpu.VMEM((4, LANES), jnp.int32),
+            pltpu.VMEM((TABLE_ROWS, 256), F32),
             pltpu.VMEM((BLOCKS * PANEL, CELLS), BF16),
             pltpu.VMEM((4 * BLOCKS, PANEL * PANEL), BF16),
-            pltpu.VMEM((4, ROWS, LANES), F32),
-            pltpu.VMEM((4, ROWS, LANES), F32),
+            pltpu.VMEM((2, ROWS, LANES), F32),
+            pltpu.VMEM((2, ROWS, LANES), F32),
+            pltpu.VMEM((2, 4 * NDEV, LANES), BF16),
+            pltpu.VMEM((2, 4 * NDEV, LANES), BF16),
             pltpu.VMEM((4, 4 * NDEV, LANES), jnp.int32),
             pltpu.VMEM((4, 4 * NDEV, LANES), jnp.int32),
             pltpu.VMEM((1024, LANES), F32),
@@ -697,7 +735,7 @@
             pltpu.SemaphoreType.DMA((8,)),
             pltpu.SemaphoreType.DMA((32,)),
             pltpu.SemaphoreType.DMA,
-            pltpu.SemaphoreType.DMA,
+            pltpu.SemaphoreType.DMA((8,)),
             pltpu.SemaphoreType.DMA,
             pltpu.SemaphoreType.DMA((4,)),
             pltpu.SemaphoreType.DMA((4,)),
@@ -707,16 +745,15 @@
     )(
         charges.reshape(64, LANES), target.reshape(64, LANES),
         stencil.reshape(BLOCKS * PANEL, CELLS), near_matrix, green.T,
-        block_dest.reshape(1, BLOCKS), block_tile.reshape(1, BLOCKS), near_offset.T, *tables,
+        block_dest.reshape(1, BLOCKS), block_tile.reshape(1, BLOCKS), near_offset.T, table,
     )
-    return (pot.reshape(-1), grad.reshape(-1))
+    return (out[:64].reshape(-1), out[64:].reshape(-1))
 
 
 def solution(mesh):
-    made = make_tables()
-    tables = [jnp.asarray(made[name]) for name in TABLES]
+    table = jnp.asarray(make_tables())
     return jax.shard_map(
-        functools.partial(local, tables),
+        functools.partial(local, table),
         mesh=mesh,
         in_specs=(
             P(("panel", "slab")),

time: 88.5 us -> 84.9 us (0.959)
  Pallas kernels: 84.8 us -> 82.7 us
  local copies, waits for them, and re-layouts: 2.75 us -> 1.4 us
    unnamed x2 -> x0, local copies, waits for them, and re-layouts: 2.75 us -> none
    pallas_call x1, Pallas kernels: 84.8 us -> 82.7 us  [local(): pl.pallas_call(kernel, out_shape=jax.ShapeDtypeStruct((128, LANES), F32),...]
    reshape x0 -> x1, local copies, waits for them, and re-layouts: none -> 1.4 us  [local(): return (out[:64].reshape(-1), out[64:].reshape(-1))]
where the time goes in v3:
time: 84.9 us; the launch traced here: 84.7 us
  Pallas kernels  82.7 us (97%)
  local copies, waits for them, and re-layouts  1.4 us (2%)
    pallas_call x1, Pallas kernels, local(): pl.pallas_call(kernel, out_shape=jax.ShapeDtypeStruct((128, LANES), F32),...  82.7 us

profile of v3, /device:TPU:1, one launch (start us, length us, event | category | flops | bytes accessed | tf_op | source)
XLA Modules:
  0.0 84.7 jit_solution(17120281077355509062)
XLA Ops:
  0.6 82.7 %panel_solver.1 = f32[128,128]{1,0:T(8,128)} custom-call(bf16[64,128]{1,0:T(8,128)(2,1)} %bitcast.14, f32[64,128]{1,0:T(8,128)} %bitcast.13, bf16[8192,256]{1,0:T(8,128)(2,1)} %bitcast.11, bf16[128,4,4096]{2,1,0:T(4,128)(2,1)} %near_hbm.1, f32[32,4096]{1,0:T(8,128)} %bitcast.12, s32[1,128]{1,0:T(1,128)} %bitcast.16, s32[1,128]{1,0:T(1,128)} %bitcast.17, ...), custom_call_target="tpu_custom_call" | custom-call | tf_op jit(solution)/shard_map/panel_solver/pallas_call | solution.py:696
  83.3 1.4 %slice_bitcast_fusion = (f32[8192]{0:T(1024)}, f32[8192]{0:T(1024)}) fusion(f32[128,128]{1,0:T(8,128)} %panel_solver.1), kind=kLoop, calls=%fused_computation | loop fusion | bytes 131072 | tf_op jit(solution)/shard_map/reshape | solution.py:750

commit v4 on v3

--- a/solution.py
+++ b/solution.py
@@ -19,12 +19,13 @@
 CELLS = 256
 LANES = 128
 MSG = 8
+GREEN_UNIT = 8191.0
 ROWS = NDEV * MSG
 MESH = pl.DeviceIdType.MESH
 F32 = jnp.float32
 BF16 = jnp.bfloat16
-TABLES = (("w1", 256), ("m0", 256), ("m0i", 256), ("w2", 128), ("a1", 128), ("w3", 128), ("t2", 128),
-          ("c0", 128), ("c1", 128), ("s0", 128), ("s1", 128), ("tm", 8))
+TABLES = (("w1", 256), ("m0", 256), ("m0i", 256), ("w2", 128), ("a1", 128), ("w3", 512), ("w5", 128), ("t2", 128),
+          ("c0", 128), ("c1", 128), ("s0", 128), ("s1", 128))
 START = {name: sum(n for _, n in TABLES[:i]) for i, (name, _) in enumerate(TABLES)}
 TABLE_ROWS = sum(n for _, n in TABLES)
 
@@ -63,18 +64,25 @@
     out["m0i"] = big.reshape(256, 256).T
     th = angle(np.arange(128), np.arange(128), 128)
     out["a1"] = np.concatenate([np.cos(th), np.sin(th)], 1)
-    th = angle(np.arange(8), np.arange(8), 8)
-    out["w3"] = np.concatenate([np.kron(np.cos(th), np.eye(16)), np.kron(np.sin(th), np.eye(16))], 1)
+    parts = []
+    for m in range(4):
+        th = angle(np.arange(8), m + 4 * np.arange(8), 32)
+        parts.append(
+            np.concatenate([np.kron(np.cos(th), np.eye(16)), np.kron(np.sin(th), np.eye(16))], 1)
+        )
+    out["w3"] = np.concatenate(parts, 0)
+    w5 = np.zeros((2, 8, 16, 8, 16))
+    for m in range(4):
+        for j in range(4):
+            th = angle(m + 4 * np.arange(8), 8 * j + np.arange(8), 32)
+            w5[0, :, m, :, j], w5[1, :, m, :, j] = np.cos(th), np.sin(th)
+    out["w5"] = np.concatenate([w5[0].reshape(128, 128), w5[1].reshape(128, 128)], 1)
     th = np.tile(angle(np.arange(128), np.arange(16), GRID), (1, 8))
     th[0] = 0.0
     out["t2"] = np.concatenate([np.cos(th), np.sin(th)], 1)
     th = np.repeat(angle(np.arange(128), np.arange(32), GRID), 16, axis=1)
     out["c0"], out["c1"] = np.cos(th[:, :256]), np.cos(th[:, 256:])
     out["s0"], out["s1"] = np.sin(th[:, :256]), np.sin(th[:, 256:])
-    th = np.repeat(angle(np.arange(4), np.arange(8), 32), 16, axis=1)
-    tm = np.zeros((8, 256))
-    tm[:4] = np.concatenate([np.cos(th), np.sin(th)], 1)
-    out["tm"] = tm
     return np.concatenate([out[name] for name, _ in TABLES], 0).astype(np.float32)
 
 
@@ -143,7 +151,7 @@
     q_hbm, target_hbm, stencil_hbm, near_hbm, green_hbm, dest_hbm, tile_hbm, offset_hbm, table_hbm,
     out_ref,
     q_ref, target_ref, green_ref, dest_ref, tile_ref, offset_ref, table,
-    stencil, near_mat, sbuf, rbuf, sback, rback, swords, rwords, gsend, grecv, ga, gb, val, charge, goal, tv,
+    stencil, near_mat, sbuf, rbuf, sback, rback, swords, rwords, gsend, grecv, ga, gb5, t5, val, charge, goal, tv,
     wf, wi, mats, xs, acc, near, ext, halo, rim,
     send_sem, recv_sem, gsend_sem, grecv_sem, load_sem, near_sem, halo_sem, rim_sem,
 ):
@@ -226,6 +234,14 @@
     def mat(slot):
         return mats[2 * slot], mats[2 * slot + 1]
 
+    every16 = lanes128 % 16 == 0
+
+    def squeeze(tiles):
+        total = jnp.where(every16, tiles[0], 0.0)
+        for j in range(1, 4):
+            total = total + pltpu.roll(jnp.where(every16, tiles[j], 0.0), j, 1)
+        return total
+
     def split_tables():
         def circle(name):
             return half_at(name, 0), half_at(name, 1)
@@ -239,9 +255,16 @@
         c, s = circle("a1")
         pair(5, cat([cat([c, s], 1), cat([-s, c], 1)], 0))
         pair(6, cat([cat([c, -s], 1), cat([s, c], 1)], 0))
-        c, s = circle("w3")
-        pair(7, cat([cat([c, -s], 1), cat([s, c], 1)], 0))
-        pair(8, cat([cat([c, s], 1), cat([-s, c], 1)], 0))
+        for m in range(4):
+            base = START["w3"] + 128 * m
+            c, s = table[base:base + 128, :LANES], table[base:base + 128, LANES:]
+            pair(7 + m, cat([cat([c, -s], 1), cat([s, c], 1)], 0))
+            c, s = c.T, s.T
+            pair(11 + m, cat([cat([c, s], 1), cat([-s, c], 1)], 0))
+        c, s = circle("w5")
+        pair(15, cat([cat([c, s], 1), cat([-s, c], 1)], 0))
+        t5[:, :LANES] = squeeze([half_at("c%d" % (j // 2), j % 2) for j in range(4)])
+        t5[:, LANES:] = squeeze([half_at("s%d" % (j // 2), j % 2) for j in range(4)])
 
     loads["dest"].wait()
     loads["tile"].wait()
@@ -384,7 +407,11 @@
             copy.start()
 
     def pack(kk, carry):
-        gsend[pl.ds(kk, 32, stride=32), :] = green_ref[:, pl.ds(pl.multiple_of(kk * LANES, LANES), LANES)]
+        def code(at):
+            x = green_ref[:, pl.ds(pl.multiple_of(at * LANES, LANES), LANES)]
+            return (x * GREEN_UNIT + 0.5).astype(jnp.int32)
+
+        gsend[pl.ds(kk, 32, stride=16), :] = (code(kk + 16) << 16) | code(kk)
         return carry
 
     def green_copies():
@@ -402,8 +429,8 @@
             slot_zero = (1 - upper) * k2 + upper * (1 - beyond) * 16 + beyond * (32 - k2)
             slot_mid = (1 - upper) * (8 + k2) + upper * (39 - k2)
             slot = (low - is_zero) * k2 + is_zero * slot_zero + is_mid * slot_mid + high * (31 - k2)
-            src = gsend.at[pl.ds(pl.multiple_of(j * 32, 32), 32)]
-            dst = grecv.at[pl.ds(pl.multiple_of(slot * 32, 32), 32)]
+            src = gsend.at[pl.ds(pl.multiple_of(j * 16, 16), 16)]
+            dst = grecv.at[pl.ds(pl.multiple_of(slot * 16, 16), 16)]
 
             @pl.when(target_dev != me)
             def _():
@@ -429,7 +456,7 @@
 
             @pl.when(target_dev != me)
             def _():
-                part = pl.ds(pl.multiple_of(j * 32, 32), 32)
+                part = pl.ds(pl.multiple_of(j * 16, 16), 16)
                 pltpu.make_async_copy(gsend.at[part], grecv.at[part], gsend_sem.at[j]).wait()
 
             return carry
@@ -438,17 +465,22 @@
 
     def green_ready():
         pltpu.make_async_copy(gsend, grecv, grecv_sem).wait()
-        scale = 2.0 ** -24
+        scale = 2.0 ** -24 / GREEN_UNIT
         flip = jnp.where((rows128 + lanes128 == 128) & (rows128 > 0), one, zero).astype(BF16)
         first = jnp.where((rows128 == 0) & (lanes128 == 0), one, zero).astype(BF16)
         eye = jnp.where(rows128 == lanes128, one, zero).astype(BF16)
         turn = cat([flip, first], 1)
-        special = (lanes128 % 16 == 0) & (me == 0)
+        special = every16 & (me == 0)
 
         def rows_of(base, kappa):
-            return cat(
-                [grecv[pl.ds(base * 32 + kappa(n), 16, stride=32), :] for n in range(8)], 0
-            )
+            rows = []
+            for n in range(8):
+                k = kappa(n)
+                words = grecv[pl.ds(base * 16 + k % 16, 16, stride=16), :]
+                rows.append(((words >> 16 if k >= 16 else words) & 65535).astype(F32))
+            return cat(rows, 0)
+
+        nyquist = []
 
         for m in range(4):
             def plain(base):
@@ -463,7 +495,8 @@
 
             d, dr, o, orr = plain(0), turned(0), plain(16), turned(16)
             ga[:, m * LANES:(m + 1) * LANES] = (d + jnp.where(special, dr, orr)) * scale
-            gb[:, m * LANES:(m + 1) * LANES] = (jnp.where(special, o, d) + orr) * scale
+            nyquist.append((o + orr) * scale)
+        gb5[...] = squeeze(nyquist)
 
     lane64 = iota((128, 128), 1) // 64
     row16 = iota((128, 128), 0) % 16
@@ -529,7 +562,7 @@
             for copy in halo_copies:
                 copy.start()
             loads["green"].wait()
-            lax.fori_loop(0, 32, pack, 0)
+            lax.fori_loop(0, 16, pack, 0)
             green_copies()
             lax.fori_loop(0, BLOCKS, near_load, 0)
             loads["table"].wait()
@@ -597,38 +630,34 @@
         er, ei, dr, di = r[0] + r[2], i[0] + i[2], r[0] - r[2], i[0] - i[2]
         fr, fi, hr, hi_ = r[1] + r[3], i[1] + i[3], r[1] - r[3], i[1] - i[3]
         vs = [(er + fr, ei + fi), (dr + hi_, di - hr), (er - fr, ei - fi), (dr - hi_, di + hr)]
-        parts = []
+        spectrum = [dot3(split(cat(list(vs[m]), 1)), mat(7 + m)) for m in range(4)]
+        vs = []
         for m in range(4):
-            cm, sm = half_at("tm", 0)[m:m + 1], half_at("tm", 1)[m:m + 1]
-            parts.append(cat(list(cmul(vs[m][0], vs[m][1], cm, sm)), 1))
-        f = dot3(split(cat(parts, 0)), mat(7))
-        both = []
-        for g in (ga, gb):
-            for m in range(4):
-                gm = g[:, m * LANES:(m + 1) * LANES]
-                fm = f[128 * m:128 * m + 128]
-                both.append(cat([fm[:, :LANES] * gm, fm[:, LANES:] * gm], 1))
-        p = dot3(split(cat(both, 0)), mat(8))
-        stacked = []
-        for e in range(2):
-            vs = []
-            for m in range(4):
-                cm, sm = half_at("tm", 0)[m:m + 1], half_at("tm", 1)[m:m + 1]
-                pm = p[512 * e + 128 * m:512 * e + 128 * m + 128]
-                vs.append(cmul_conj(pm[:, :LANES], pm[:, LANES:], cm, sm))
-            r = [v[0] for v in vs]
-            i = [v[1] for v in vs]
-            er, ei, dr, di = r[0] + r[2], i[0] + i[2], r[0] - r[2], i[0] - i[2]
-            fr, fi, hr, hi_ = r[1] + r[3], i[1] + i[3], r[1] - r[3], i[1] - i[3]
-            zs = [(er + fr, ei + fi), (dr - hi_, di + hr), (er - fr, ei - fi), (dr + hi_, di - hr)]
-            re, im = cmul_conj(
-                cat([z[0] for z in zs], 1), cat([z[1] for z in zs], 1), c1, s1,
-            )
-            stacked.append(split(cat([re, im], 0)))
-        inv = mat(6)
-        yr = dot3((inv[0][:128], inv[1][:128]), stacked[0])
-        yi = dot3((inv[0][128:], inv[1][128:]), stacked[1])
-        put_words(inv_, [lane_tile(yr, j) for j in range(4)], [lane_tile(yi, j) for j in range(4)])
+            gm = ga[:, m * LANES:(m + 1) * LANES]
+            p = dot3(split(spectrum[m] * cat([gm, gm], 1)), mat(11 + m))
+            vs.append((p[:, :LANES], p[:, LANES:]))
+        r = [v[0] for v in vs]
+        i = [v[1] for v in vs]
+        er, ei, dr, di = r[0] + r[2], i[0] + i[2], r[0] - r[2], i[0] - i[2]
+        fr, fi, hr, hi_ = r[1] + r[3], i[1] + i[3], r[1] - r[3], i[1] - i[3]
+        zs = [(er + fr, ei + fi), (dr - hi_, di + hr), (er - fr, ei - fi), (dr + hi_, di - hr)]
+        re, im = cmul_conj(cat([z[0] for z in zs], 1), cat([z[1] for z in zs], 1), c1, s1)
+        y = dot3(mat(6), split(cat([re, im], 0)))
+        g5 = gb5[...]
+        p = dot3(
+            split(cat([squeeze([f[:, :LANES] for f in spectrum]) * g5,
+                       squeeze([f[:, LANES:] for f in spectrum]) * g5], 1)),
+            mat(15),
+        )
+        re, im = cmul_conj(p[:, :LANES], p[:, LANES:], t5[:, :LANES], t5[:, LANES:])
+        y5 = dot3((mats[12, 128:, :], mats[13, 128:, :]), split(cat([re, im], 0)))
+        here = every16 & (me == 0)
+        yr = [lane_tile(y[:128], j) for j in range(4)]
+        yi = [
+            jnp.where(here, pltpu.roll(y5, LANES - j, 1) if j else y5, lane_tile(y[128:], j))
+            for j in range(4)
+        ]
+        put_words(inv_, yr, yi)
         exchange(step0 + 2, swords.at[inv_], rwords.at[inv_], 4, 4)
 
         @pl.when(first)
@@ -696,7 +725,7 @@
     out = pl.pallas_call(
         kernel,
         out_shape=jax.ShapeDtypeStruct((128, LANES), F32),
-        in_specs=[pl.BlockSpec(memory_space=pl.ANY)] * 9,
+        in_specs=[pl.BlockSpec(memory_space=pltpu.HBM)] * 9,
         out_specs=pl.BlockSpec(memory_space=pltpu.VMEM),
         scratch_shapes=[
             pltpu.VMEM((64, LANES), BF16),
@@ -714,17 +743,18 @@
             pltpu.VMEM((2, 4 * NDEV, LANES), BF16),
             pltpu.VMEM((4, 4 * NDEV, LANES), jnp.int32),
             pltpu.VMEM((4, 4 * NDEV, LANES), jnp.int32),
-            pltpu.VMEM((1024, LANES), F32),
-            pltpu.VMEM((1024, LANES), F32),
+            pltpu.VMEM((512, LANES), jnp.int32),
+            pltpu.VMEM((512, LANES), jnp.int32),
             pltpu.VMEM((128, 512), F32),
-            pltpu.VMEM((128, 512), F32),
+            pltpu.VMEM((128, LANES), F32),
+            pltpu.VMEM((128, 256), F32),
             pltpu.VMEM((128, 128), F32),
             pltpu.VMEM((128, 128), F32),
             pltpu.VMEM((128, 128), F32),
             pltpu.VMEM((128, 256), F32),
             pltpu.VMEM((4, 256, 256), BF16),
             pltpu.VMEM((2, 256, 512), BF16),
-            pltpu.VMEM((18, 256, 256), BF16),
+            pltpu.VMEM((32, 256, 256), BF16),
             pltpu.VMEM((512, LANES), F32),
             pltpu.VMEM((512, LANES), F32),
             pltpu.VMEM((128, LANES), F32),
@@ -740,7 +770,9 @@
             pltpu.SemaphoreType.DMA((4,)),
             pltpu.SemaphoreType.DMA((4,)),
         ],
-        compiler_params=pltpu.CompilerParams(collective_id=0, has_side_effects=True),
+        compiler_params=pltpu.CompilerParams(
+            collective_id=0, has_side_effects=True, vmem_limit_bytes=44 << 20
+        ),
         name="panel_solver",
     )(
         charges.reshape(64, LANES), target.reshape(64, LANES),

time: 84.9 us -> 89.6 us (1.055)
  local copies, waits for them, and re-layouts: 1.4 us -> 8.98 us
  Pallas kernels: 82.7 us -> 79.6 us
    unnamed x0 -> x16, local copies, waits for them, and re-layouts: none -> 8.35 us
    pallas_call x1, Pallas kernels: 82.7 us -> 79.6 us  [local(): pl.pallas_call(kernel, out_shape=jax.ShapeDtypeStruct((128, LANES), F32),...]
where the time goes in v4:
time: 89.6 us; the launch traced here: 89.2 us
  Pallas kernels  79.6 us (89%)
  local copies, waits for them, and re-layouts  8.98 us (10%)
    pallas_call x1, Pallas kernels, local(): pl.pallas_call(kernel, out_shape=jax.ShapeDtypeStruct((128, LANES), F32),...  79.6 us
    unnamed x16, local copies, waits for them, and re-layouts  8.35 us

profile of v4, /device:TPU:1, one launch (start us, length us, event | category | flops | bytes accessed | tf_op | source)
XLA Modules:
  0.0 89.2 jit_solution(14334493334305715224)
XLA Ops:
  0.6 0.0 copy-start
  0.6 2.2 %copy-done = bf16[128,64,256]{2,1,0:T(8,128)(2,1)S(1)} copy-done((bf16[128,64,256]{2,1,0:T(8,128)(2,1)S(1)}, bf16[128,64,256]{2,1,0:T(8,128)(2,1)}, u32[]{:S(2)}) %copy-start) | copy-done | bytes 4194328
  2.8 0.0 copy-start.1
  2.8 1.7 %copy-done.1 = f32[2304,256]{1,0:T(8,128)S(1)} copy-done((f32[2304,256]{1,0:T(8,128)S(1)}, f32[2304,256]{1,0:T(8,128)}, u32[]{:S(2)}) %copy-start.1) | copy-done | bytes 2359320
  4.5 0.0 copy-start.2
  4.5 1.0 %copy-done.2 = f32[4096,32]{0,1:T(8,128)S(1)} copy-done((f32[4096,32]{0,1:T(8,128)S(1)}, f32[4096,32]{0,1:T(8,128)}, u32[]{:S(2)}) %copy-start.2) | copy-done | bytes 524312
  5.5 0.0 copy-start.3
  5.5 0.8 copy-done.3
  6.3 0.0 copy-start.4
  6.3 0.7 copy-done.4
  7.0 0.0 copy-start.5
  7.0 0.7 copy-done.5
  7.7 0.0 copy-start.6
  7.7 0.7 copy-done.6
  8.3 0.0 copy-start.7
  8.3 0.7 copy-done.7
  9.0 79.6 %panel_solver.1 = f32[128,128]{1,0:T(8,128)S(1)} custom-call(bf16[64,128]{1,0:T(8,128)(2,1)S(1)} %bitcast.14, f32[64,128]{1,0:T(8,128)S(1)} %bitcast.13, bf16[8192,256]{1,0:T(8,128)(2,1)S(1)} %bitcast.11, bf16[128,4,4096]{2,1,0:T(4,128)(2,1)} %near_hbm.1, f32[32,4096]{1,0:T(8,128)S(1)} %bitcast.12, s32[1,128]{1,0:T(1,128)S(1)} %bitcast.16, ...), custom_call_target="tpu_custom_call" | custom-call | tf_op jit(solution)/shard_map/panel_solver/pallas_call | solution.py:725
  88.6 0.6 slice_bitcast_fusion
Async XLA Ops:
  0.6 2.2 %copy-start = (bf16[128,64,256]{2,1,0:T(8,128)(2,1)S(1)}, bf16[128,64,256]{2,1,0:T(8,128)(2,1)}, u32[]{:S(2)}) copy-start(bf16[128,64,256]{2,1,0:T(8,128)(2,1)} %param.11) | copy-start | bytes 12582916
  2.8 1.7 %copy-start.1 = (f32[2304,256]{1,0:T(8,128)S(1)}, f32[2304,256]{1,0:T(8,128)}, u32[]{:S(2)}) copy-start(f32[2304,256]{1,0:T(8,128)} %constant.2.clone.table_hbm) | copy-start | bytes 7077892
  4.5 1.0 %copy-start.2 = (f32[4096,32]{0,1:T(8,128)S(1)}, f32[4096,32]{0,1:T(8,128)}, u32[]{:S(2)}) copy-start(f32[4096,32]{0,1:T(8,128)} %param.13) | copy-start | bytes 1572868
  5.5 0.8 copy-start.3
  6.3 0.7 copy-start.4
  7.0 0.7 copy-start.5
  7.7 0.7 copy-start.6
  8.3 0.7 copy-start.7

commit v5 on v4

--- a/solution.py
+++ b/solution.py
@@ -725,7 +725,7 @@
     out = pl.pallas_call(
         kernel,
         out_shape=jax.ShapeDtypeStruct((128, LANES), F32),
-        in_specs=[pl.BlockSpec(memory_space=pltpu.HBM)] * 9,
+        in_specs=[pl.BlockSpec(memory_space=pl.ANY)] * 9,
         out_specs=pl.BlockSpec(memory_space=pltpu.VMEM),
         scratch_shapes=[
             pltpu.VMEM((64, LANES), BF16),
@@ -770,9 +770,7 @@
             pltpu.SemaphoreType.DMA((4,)),
             pltpu.SemaphoreType.DMA((4,)),
         ],
-        compiler_params=pltpu.CompilerParams(
-            collective_id=0, has_side_effects=True, vmem_limit_bytes=44 << 20
-        ),
+        compiler_params=pltpu.CompilerParams(collective_id=0, has_side_effects=True),
         name="panel_solver",
     )(
         charges.reshape(64, LANES), target.reshape(64, LANES),

time: 89.6 us -> 82 us (0.915)
  local copies, waits for them, and re-layouts: 8.98 us -> 1.4 us
    unnamed x16 -> x0, local copies, waits for them, and re-layouts: 8.35 us -> none
where the time goes in v5:
time: 82 us; the launch traced here: 81.8 us
  Pallas kernels  79.8 us (97%)
  local copies, waits for them, and re-layouts  1.4 us (2%)
    pallas_call x1, Pallas kernels, local(): pl.pallas_call(kernel, out_shape=jax.ShapeDtypeStruct((128, LANES), F32),...  79.8 us

profile of v5, /device:TPU:1, one launch (start us, length us, event | category | flops | bytes accessed | tf_op | source)
XLA Modules:
  0.0 81.8 jit_solution(11567172633135483114)
XLA Ops:
  0.6 79.8 %panel_solver.1 = f32[128,128]{1,0:T(8,128)} custom-call(bf16[64,128]{1,0:T(8,128)(2,1)} %bitcast.14, f32[64,128]{1,0:T(8,128)} %bitcast.13, bf16[8192,256]{1,0:T(8,128)(2,1)} %bitcast.11, bf16[128,4,4096]{2,1,0:T(4,128)(2,1)} %near_hbm.1, f32[32,4096]{1,0:T(8,128)} %bitcast.12, s32[1,128]{1,0:T(1,128)} %bitcast.16, s32[1,128]{1,0:T(1,128)} %bitcast.17, ...), custom_call_target="tpu_custom_call" | custom-call | tf_op jit(solution)/shard_map/panel_solver/pallas_call | solution.py:725
  80.4 1.4 %slice_bitcast_fusion = (f32[8192]{0:T(1024)}, f32[8192]{0:T(1024)}) fusion(f32[128,128]{1,0:T(8,128)} %panel_solver.1), kind=kLoop, calls=%fused_computation | loop fusion | bytes 131072 | tf_op jit(solution)/shard_map/reshape | solution.py:780

commit v6 on v5

--- a/solution.py
+++ b/solution.py
@@ -18,9 +18,7 @@
 PANEL = 64
 CELLS = 256
 LANES = 128
-MSG = 8
 GREEN_UNIT = 8191.0
-ROWS = NDEV * MSG
 MESH = pl.DeviceIdType.MESH
 F32 = jnp.float32
 BF16 = jnp.bfloat16
@@ -100,7 +98,9 @@
 
 
 def dot3(a, b):
-    return dot(a[0], b[0]) + (dot(a[0], b[1]) + dot(a[1], b[0]))
+    n = a[0].shape[0]
+    both = dot(jnp.concatenate(a, 0), b[0])
+    return both[:n] + (both[n:] + dot(a[0], b[1]))
 
 
 def iota(shape, dim):
@@ -147,11 +147,37 @@
     return re, im
 
 
+def encode_pairs(values):
+    flat = [x for pair in values for x in pair]
+    top = jnp.abs(flat[0])
+    for x in flat[1:]:
+        top = jnp.maximum(top, jnp.abs(x))
+    power = jnp.floor(jnp.log2(jnp.maximum(top, 2.0 ** -100))) + 1.0
+    scale = jnp.exp2(13.0 - power)
+    code = power.astype(jnp.int32) + 128
+
+    def mantissa(x):
+        return jnp.minimum(x * scale + 8192.5, 16383.5).astype(jnp.int32)
+
+    return [
+        (((code >> (4 * k)) & 15) << 28) | (mantissa(a) << 14) | mantissa(b)
+        for k, (a, b) in enumerate(values)
+    ]
+
+
+def decode_pairs(words):
+    code = (words[0] >> 28 & 15) | ((words[1] >> 28 & 15) << 4)
+    scale = jnp.exp2(code.astype(F32) - 141.0)
+    return [
+        [((w >> at & 16383).astype(F32) - 8192.0) * scale for at in (14, 0)] for w in words
+    ]
+
+
 def kernel(
     q_hbm, target_hbm, stencil_hbm, near_hbm, green_hbm, dest_hbm, tile_hbm, offset_hbm, table_hbm,
     out_ref,
     q_ref, target_ref, green_ref, dest_ref, tile_ref, offset_ref, table,
-    stencil, near_mat, sbuf, rbuf, sback, rback, swords, rwords, gsend, grecv, ga, gb5, t5, val, charge, goal, tv,
+    stencil, near_mat, sback, rback, swords, rwords, gsend, grecv, ga, gb5, t5, val, charge, goal, tv,
     wf, wi, mats, xs, acc, near, ext, halo, rim,
     send_sem, recv_sem, gsend_sem, grecv_sem, load_sem, near_sem, halo_sem, rim_sem,
 ):
@@ -159,6 +185,36 @@
     slab = lax.axis_index("slab")
     me = panel * SLABS + slab
     pz, px, pc = panel // 8, (panel // 2) % 4, panel % 2
+
+    def rows_at(name):
+        n = dict(TABLES)[name]
+        return table[START[name]:START[name] + n, :]
+
+    def half_at(name, half):
+        n = dict(TABLES)[name]
+        return table[START[name]:START[name] + n, half * LANES:(half + 1) * LANES]
+
+    def others(visit):
+        def body(g, carry):
+            z = (pz + ((Z_DIGITS >> (2 * g)) & 3)) % 4
+            x = (px + ((X_DIGITS >> (2 * g)) & 3)) % 4
+            for dy in (2, 1, 3, 0):
+                for dc in (1, 0):
+                    def go(z=z, x=x, dy=dy, dc=dc):
+                        visit(z * 8 + x * 2 + (pc + dc) % 2, (slab + dy) % 4)
+
+                    if dy == 0 and dc == 0:
+                        pl.when(g != 15)(go)
+                    else:
+                        go()
+            return carry
+
+        lax.fori_loop(0, 16, body, 0)
+
+    barrier = pltpu.get_barrier_semaphore()
+    others(
+        lambda p, y: pl.semaphore_signal(barrier, inc=1, device_id=(p, y), device_id_type=MESH)
+    )
 
     loads = {}
     for i, (name, src, dst) in enumerate((
@@ -169,36 +225,6 @@
     )):
         loads[name] = pltpu.make_async_copy(src, dst, load_sem.at[i])
         loads[name].start()
-
-    def rows_at(name):
-        n = dict(TABLES)[name]
-        return table[START[name]:START[name] + n, :]
-
-    def half_at(name, half):
-        n = dict(TABLES)[name]
-        return table[START[name]:START[name] + n, half * LANES:(half + 1) * LANES]
-
-    def others(visit):
-        def body(g, carry):
-            z = (pz + ((Z_DIGITS >> (2 * g)) & 3)) % 4
-            x = (px + ((X_DIGITS >> (2 * g)) & 3)) % 4
-            for dy in (2, 1, 3, 0):
-                for dc in (1, 0):
-                    def go(z=z, x=x, dy=dy, dc=dc):
-                        visit(z * 8 + x * 2 + (pc + dc) % 2, (slab + dy) % 4)
-
-                    if dy == 0 and dc == 0:
-                        pl.when(g != 15)(go)
-                    else:
-                        go()
-            return carry
-
-        lax.fori_loop(0, 16, body, 0)
-
-    barrier = pltpu.get_barrier_semaphore()
-    others(
-        lambda p, y: pl.semaphore_signal(barrier, inc=1, device_id=(p, y), device_id_type=MESH)
-    )
 
     def near_load(b, carry):
         pltpu.make_async_copy(
@@ -313,18 +339,18 @@
         part = pl.ds(0, (NDEV - 1) * count)
         pltpu.make_async_copy(src.at[part], dst.at[part], send_sem.at[step]).wait()
 
-    def put(slot, row, value):
-        sbuf[slot, pl.ds(row, NDEV, stride=MSG), :] = value
-
-    def get(slot, row):
-        return rbuf[slot, pl.ds(row, NDEV, stride=MSG), :]
+    def put_row(slot, row, value):
+        swords[slot, pl.ds(row, NDEV, stride=4), :] = value
+
+    def get_row(slot, row):
+        return rwords[slot, pl.ds(row, NDEV, stride=4), :]
 
     def put_words(slot, re, im):
         for j, w in enumerate(encode(re, im)):
-            swords[slot, pl.ds(j, NDEV, stride=4), :] = w
+            put_row(slot, j, w)
 
     def get_words(slot):
-        return decode([rwords[slot, pl.ds(j, NDEV, stride=4), :] for j in range(4)])
+        return decode([get_row(slot, j) for j in range(4)])
 
     def next_to(shift):
         other = (me + shift + NDEV) % NDEV
@@ -550,15 +576,17 @@
         first, last = which == 0, which == 1
         fwd, inv_ = which * 2, which * 2 + 1
         out = project()
+        coded = encode_pairs(
+            [[lane_tile(out[128 * k:128 * k + 128], h) for h in range(2)] for k in range(2)]
+        )
         for k in range(2):
-            for h in range(2):
-                put(which, 2 * k + h, lane_tile(out[128 * k:128 * k + 128], h))
+            put_row(4 + which, k, coded[k])
 
         @pl.when(first)
         def _():
-            put(0, 4, id_rows)
+            put_row(4, 2, id_rows.astype(jnp.int32))
             pl.semaphore_wait(barrier, NDEV - 1)
-            exchange(0, sbuf.at[0], rbuf.at[0], MSG, 5)
+            exchange(0, swords.at[4], rwords.at[4], 4, 3)
             for copy in halo_copies:
                 copy.start()
             loads["green"].wait()
@@ -569,16 +597,18 @@
             split_tables()
             loads["target"].wait()
             unfold(target_ref, goal)
-            arrived(0, sbuf.at[0], rbuf.at[0], 5)
-            idm = get(0, 4)
+            arrived(0, swords.at[4], rwords.at[4], 3)
+            idm = get_row(4, 2)
             tc = iota((128, 256), 1)
             for k in range(2):
-                xs[pl.ds(k, 128, stride=2), :] = jnp.broadcast_to(idm[:, k:k + 1], (128, 128))
+                xs[pl.ds(k, 128, stride=2), :] = jnp.broadcast_to(
+                    idm[:, k:k + 1].astype(F32), (128, 128)
+                )
             ordered = xs[:256, :1].astype(jnp.int32)
             for tr in range(2):
                 pick = cat(
                     [
-                        jnp.where(idm[:, k:k + 1].astype(jnp.int32) == tc + (tr * 256 + 1), one, zero)
+                        jnp.where(idm[:, k:k + 1] == tc + (tr * 256 + 1), one, zero)
                         for k in range(2)
                     ],
                     0,
@@ -592,13 +622,12 @@
 
         @pl.when(last)
         def _():
-            exchange(4, sbuf.at[1], rbuf.at[1], MSG, 4)
+            exchange(4, swords.at[5], rwords.at[5], 4, 2)
             near_adjoint()
-            arrived(4, sbuf.at[1], rbuf.at[1], 4)
-
-        tiles = split(
-            cat([cat([get(which, 2 * k + h) for h in range(2)], 1) for k in range(2)], 0)
-        )
+            arrived(4, swords.at[5], rwords.at[5], 2)
+
+        values = decode_pairs([get_row(4 + which, k) for k in range(2)])
+        tiles = split(cat([cat(v, 1) for v in values], 0))
         c2, s2 = half_at("t2", 0), half_at("t2", 1)
         c1 = cat([rows_at("c0"), rows_at("c1")], 1)
         s1 = cat([rows_at("s0"), rows_at("s1")], 1)
@@ -712,7 +741,7 @@
 
     lax.fori_loop(0, 2, both_passes, 0)
     for p in range(2):
-        sent(4 * p, sbuf.at[p], rbuf.at[p], 5 - p)
+        sent(4 * p, swords.at[4 + p], rwords.at[4 + p], 3 - p)
         sent(4 * p + 1, swords.at[2 * p], rwords.at[2 * p], 4)
         sent(4 * p + 2, swords.at[2 * p + 1], rwords.at[2 * p + 1], 4)
         sent(4 * p + 3, sback.at[p], rback.at[p], 4)
@@ -737,12 +766,10 @@
             pltpu.VMEM((TABLE_ROWS, 256), F32),
             pltpu.VMEM((BLOCKS * PANEL, CELLS), BF16),
             pltpu.VMEM((4 * BLOCKS, PANEL * PANEL), BF16),
-            pltpu.VMEM((2, ROWS, LANES), F32),
-            pltpu.VMEM((2, ROWS, LANES), F32),
             pltpu.VMEM((2, 4 * NDEV, LANES), BF16),
             pltpu.VMEM((2, 4 * NDEV, LANES), BF16),
-            pltpu.VMEM((4, 4 * NDEV, LANES), jnp.int32),
-            pltpu.VMEM((4, 4 * NDEV, LANES), jnp.int32),
+            pltpu.VMEM((6, 4 * NDEV, LANES), jnp.int32),
+            pltpu.VMEM((6, 4 * NDEV, LANES), jnp.int32),
             pltpu.VMEM((512, LANES), jnp.int32),
             pltpu.VMEM((512, LANES), jnp.int32),
             pltpu.VMEM((128, 512), F32),

time: 82 us -> 79.8 us (0.973)
  Pallas kernels: 79.8 us -> 77.6 us
    pallas_call x1, Pallas kernels: 79.8 us -> 77.6 us  [local(): pl.pallas_call(kernel, out_shape=jax.ShapeDtypeStruct((128, LANES), F32),...]
where the time goes in v6:
time: 79.8 us; the launch traced here: 79.6 us
  Pallas kernels  77.6 us (97%)
  local copies, waits for them, and re-layouts  1.4 us (2%)
    pallas_call x1, Pallas kernels, local(): pl.pallas_call(kernel, out_shape=jax.ShapeDtypeStruct((128, LANES), F32),...  77.6 us

profile of v6, /device:TPU:1, one launch (start us, length us, event | category | flops | bytes accessed | tf_op | source)
XLA Modules:
  0.0 79.6 jit_solution(9114430637097296195)
XLA Ops:
  0.6 77.6 %panel_solver.1 = f32[128,128]{1,0:T(8,128)} custom-call(bf16[64,128]{1,0:T(8,128)(2,1)} %bitcast.14, f32[64,128]{1,0:T(8,128)} %bitcast.13, bf16[8192,256]{1,0:T(8,128)(2,1)} %bitcast.11, bf16[128,4,4096]{2,1,0:T(4,128)(2,1)} %near_hbm.1, f32[32,4096]{1,0:T(8,128)} %bitcast.12, s32[1,128]{1,0:T(1,128)} %bitcast.16, s32[1,128]{1,0:T(1,128)} %bitcast.17, ...), custom_call_target="tpu_custom_call" | custom-call | tf_op jit(solution)/shard_map/panel_solver/pallas_call | solution.py:754
  78.2 1.4 %slice_bitcast_fusion = (f32[8192]{0:T(1024)}, f32[8192]{0:T(1024)}) fusion(f32[128,128]{1,0:T(8,128)} %panel_solver.1), kind=kLoop, calls=%fused_computation | loop fusion | bytes 131072 | tf_op jit(solution)/shard_map/reshape | solution.py:807

commit v7 on v6

--- a/solution.py
+++ b/solution.py
@@ -177,8 +177,8 @@
     q_hbm, target_hbm, stencil_hbm, near_hbm, green_hbm, dest_hbm, tile_hbm, offset_hbm, table_hbm,
     out_ref,
     q_ref, target_ref, green_ref, dest_ref, tile_ref, offset_ref, table,
-    stencil, near_mat, sback, rback, swords, rwords, gsend, grecv, ga, gb5, t5, val, charge, goal, tv,
-    wf, wi, mats, xs, acc, near, ext, halo, rim,
+    stencil, turned, near_mat, sback, rback, swords, rwords, gsend, grecv, ga, gb5, t5, val, charge, goal, tv,
+    wf, wi, mats, xs, order, acc, near, ext, halo, rim,
     send_sem, recv_sem, gsend_sem, grecv_sem, load_sem, near_sem, halo_sem, rim_sem,
 ):
     panel = lax.axis_index("panel")
@@ -387,6 +387,7 @@
         pltpu.make_async_copy(near_mat, near_mat, near_sem).wait()
         acc[...] = jnp.zeros((512, 128), F32)
 
+    def near_products(begin, end):
         def body(c, carry):
             col = pl.ds(pl.multiple_of(c * 256, 256), 256)
             gather = jnp.where(
@@ -399,8 +400,7 @@
                 acc[row, :] = acc[row, :] + (dot(hi, gather) + dot(lo, gather))
             return carry
 
-        lax.fori_loop(0, 16, body, 0)
-        near[...] = sum(acc[pl.ds(k, 128, stride=4), :] for k in range(4))
+        lax.fori_loop(begin, end, body, 0)
 
     def near_adjoint():
         for k in range(4):
@@ -431,6 +431,30 @@
         ext[...] = total
         for copy in rim_copies:
             copy.start()
+
+    def back_table():
+        idm = get_row(4, 2)
+        for k in range(2):
+            xs[pl.ds(k, 128, stride=2), :] = jnp.broadcast_to(
+                idm[:, k:k + 1].astype(F32), (128, 128)
+            )
+        ordered = xs[:256, :1].astype(jnp.int32)
+        for tr in range(2):
+            pick = jnp.where(
+                ordered == iota((256, 256), 1) + (tr * 256 + 1), one, zero
+            ).astype(BF16)
+            for t in range(2):
+                wi[t, :, tr * 256:(tr + 1) * 256] = dot_nt(pick, mats[t]).astype(BF16)
+
+    def turn_stencil():
+        eye = jnp.where(iota((256, 256), 0) == iota((256, 256), 1), one, zero).astype(BF16)
+
+        def body(g, carry):
+            at = pl.multiple_of(g * 512, 512)
+            turned[:, pl.ds(at, 512)] = dot_nt(eye, stencil[pl.ds(at, 512), :]).astype(BF16)
+            return carry
+
+        lax.fori_loop(0, 16, body, 0)
 
     def pack(kk, carry):
         def code(at):
@@ -542,8 +566,7 @@
         rows = []
         l64, r16 = iota((16, 128), 1) // 64, iota((16, 128), 0)
         for g in range(8):
-            part = stencil[g * 1024:(g + 1) * 1024, :]
-            r = dot_nt(own_tiles[g * 16:(g + 1) * 16, :], part)
+            r = dot(own_tiles[g * 16:(g + 1) * 16, :], turned[:, g * 1024:(g + 1) * 1024])
             acc = jnp.zeros((16, 128), F32)
             for i in range(8):
                 acc = acc + jnp.where(l64 + 2 * i == r16, r[:, i * LANES:(i + 1) * LANES], 0.0)
@@ -600,11 +623,6 @@
             arrived(0, swords.at[4], rwords.at[4], 3)
             idm = get_row(4, 2)
             tc = iota((128, 256), 1)
-            for k in range(2):
-                xs[pl.ds(k, 128, stride=2), :] = jnp.broadcast_to(
-                    idm[:, k:k + 1].astype(F32), (128, 128)
-                )
-            ordered = xs[:256, :1].astype(jnp.int32)
             for tr in range(2):
                 pick = cat(
                     [
@@ -613,12 +631,8 @@
                     ],
                     0,
                 ).astype(BF16)
-                back_pick = jnp.where(
-                    ordered == iota((256, 256), 1) + (tr * 256 + 1), one, zero
-                ).astype(BF16)
                 for t in range(2):
                     wf[2 * tr + t] = dot_nt(mats[t], pick).astype(BF16)
-                    wi[t, :, tr * 256:(tr + 1) * 256] = dot_nt(back_pick, mats[t]).astype(BF16)
 
         @pl.when(last)
         def _():
@@ -645,6 +659,8 @@
         @pl.when(first)
         def _():
             green_ready()
+            back_table()
+            turn_stencil()
 
         @pl.when(last)
         def _():
@@ -692,6 +708,7 @@
         @pl.when(first)
         def _():
             near_forward()
+            near_products(0, 9)
 
         arrived(step0 + 2, swords.at[inv_], rwords.at[inv_], 4)
         re, im = get_words(inv_)
@@ -708,9 +725,15 @@
         )
         back = dot3((wi[0], wi[1]), split(y))
         for h in range(2):
-            xs[pl.ds(h, 256, stride=2), :] = lane_tile(back, h)
-        sback[which] = xs[...].astype(BF16)
+            order[pl.ds(h, 256, stride=2), :] = lane_tile(back, h)
+        sback[which] = order[...].astype(BF16)
         exchange(step0 + 3, sback.at[which], rback.at[which], 4, 4)
+
+        @pl.when(first)
+        def _():
+            near_products(9, 16)
+            near[...] = sum(acc[pl.ds(k, 128, stride=4), :] for k in range(4))
+
         arrived(step0 + 3, sback.at[which], rback.at[which], 4)
         tiles = rback[which]
         far = interpolate(cat([dot(in_pick[h], tiles) for h in range(2)], 1).astype(BF16))
@@ -765,6 +788,7 @@
             pltpu.VMEM((4, LANES), jnp.int32),
             pltpu.VMEM((TABLE_ROWS, 256), F32),
             pltpu.VMEM((BLOCKS * PANEL, CELLS), BF16),
+            pltpu.VMEM((CELLS, BLOCKS * PANEL), BF16),
             pltpu.VMEM((4 * BLOCKS, PANEL * PANEL), BF16),
             pltpu.VMEM((2, 4 * NDEV, LANES), BF16),
             pltpu.VMEM((2, 4 * NDEV, LANES), BF16),
@@ -782,6 +806,7 @@
             pltpu.VMEM((4, 256, 256), BF16),
             pltpu.VMEM((2, 256, 512), BF16),
             pltpu.VMEM((32, 256, 256), BF16),
+            pltpu.VMEM((512, LANES), F32),
             pltpu.VMEM((512, LANES), F32),
             pltpu.VMEM((512, LANES), F32),
             pltpu.VMEM((128, LANES), F32),

time: 79.8 us -> 78.7 us (0.986)
  Pallas kernels: 77.6 us -> 76.5 us
    pallas_call x1, Pallas kernels: 77.6 us -> 76.5 us  [local(): pl.pallas_call(kernel, out_shape=jax.ShapeDtypeStruct((128, LANES), F32),...]
where the time goes in v7:
time: 78.7 us; the launch traced here: 78.5 us
  Pallas kernels  76.5 us (97%)
  local copies, waits for them, and re-layouts  1.4 us (2%)
    pallas_call x1, Pallas kernels, local(): pl.pallas_call(kernel, out_shape=jax.ShapeDtypeStruct((128, LANES), F32),...  76.5 us

profile of v7, /device:TPU:1, one launch (start us, length us, event | category | flops | bytes accessed | tf_op | source)
XLA Modules:
  0.0 78.5 jit_solution(6308138721552141032)
XLA Ops:
  0.6 76.5 %panel_solver.1 = f32[128,128]{1,0:T(8,128)} custom-call(bf16[64,128]{1,0:T(8,128)(2,1)} %bitcast.14, f32[64,128]{1,0:T(8,128)} %bitcast.13, bf16[8192,256]{1,0:T(8,128)(2,1)} %bitcast.11, bf16[128,4,4096]{2,1,0:T(4,128)(2,1)} %near_hbm.1, f32[32,4096]{1,0:T(8,128)} %bitcast.12, s32[1,128]{1,0:T(1,128)} %bitcast.16, s32[1,128]{1,0:T(1,128)} %bitcast.17, ...), custom_call_target="tpu_custom_call" | custom-call | tf_op jit(solution)/shard_map/panel_solver/pallas_call | solution.py:777
  77.1 1.4 %slice_bitcast_fusion = (f32[8192]{0:T(1024)}, f32[8192]{0:T(1024)}) fusion(f32[128,128]{1,0:T(8,128)} %panel_solver.1), kind=kLoop, calls=%fused_computation | loop fusion | bytes 131072 | tf_op jit(solution)/shard_map/reshape | solution.py:832

commit v8 on v7

--- a/solution.py
+++ b/solution.py
@@ -194,6 +194,18 @@
         n = dict(TABLES)[name]
         return table[START[name]:START[name] + n, half * LANES:(half + 1) * LANES]
 
+    loads = {
+        name: pltpu.make_async_copy(src, dst, load_sem.at[i])
+        for i, (name, src, dst) in enumerate((
+            ("q", q_hbm, q_ref), ("dest", dest_hbm, dest_ref), ("tile", tile_hbm, tile_ref),
+            ("stencil", stencil_hbm, stencil), ("table", table_hbm, table),
+            ("green", green_hbm, green_ref), ("offset", offset_hbm, offset_ref),
+            ("target", target_hbm, target_ref),
+        ))
+    }
+    for name in ("q", "dest", "tile", "stencil"):
+        loads[name].start()
+
     def others(visit):
         def body(g, carry):
             z = (pz + ((Z_DIGITS >> (2 * g)) & 3)) % 4
@@ -216,14 +228,7 @@
         lambda p, y: pl.semaphore_signal(barrier, inc=1, device_id=(p, y), device_id_type=MESH)
     )
 
-    loads = {}
-    for i, (name, src, dst) in enumerate((
-        ("q", q_hbm, q_ref), ("dest", dest_hbm, dest_ref), ("tile", tile_hbm, tile_ref),
-        ("stencil", stencil_hbm, stencil), ("table", table_hbm, table),
-        ("green", green_hbm, green_ref), ("offset", offset_hbm, offset_ref),
-        ("target", target_hbm, target_ref),
-    )):
-        loads[name] = pltpu.make_async_copy(src, dst, load_sem.at[i])
+    for name in ("table", "green", "offset", "target"):
         loads[name].start()
 
     def near_load(b, carry):
@@ -338,6 +343,12 @@
     def sent(step, src, dst, count):
         part = pl.ds(0, (NDEV - 1) * count)
         pltpu.make_async_copy(src.at[part], dst.at[part], send_sem.at[step]).wait()
+
+    def pass_sent(p):
+        sent(4 * p, swords.at[4 + p], rwords.at[4 + p], 3 - p)
+        sent(4 * p + 1, swords.at[2 * p], rwords.at[2 * p], 4)
+        sent(4 * p + 2, swords.at[2 * p + 1], rwords.at[2 * p + 1], 4)
+        sent(4 * p + 3, sback.at[p], rback.at[p], 4)
 
     def put_row(slot, row, value):
         swords[slot, pl.ds(row, NDEV, stride=4), :] = value
@@ -665,6 +676,10 @@
         @pl.when(last)
         def _():
             near_scatter()
+            green_sent()
+            pass_sent(0)
+            for copy in halo_copies:
+                copy.wait_send()
 
         arrived(step0 + 1, swords.at[fwd], rwords.at[fwd], 4)
         re, im = get_words(fwd)
@@ -763,13 +778,8 @@
         return carry
 
     lax.fori_loop(0, 2, both_passes, 0)
-    for p in range(2):
-        sent(4 * p, swords.at[4 + p], rwords.at[4 + p], 3 - p)
-        sent(4 * p + 1, swords.at[2 * p], rwords.at[2 * p], 4)
-        sent(4 * p + 2, swords.at[2 * p + 1], rwords.at[2 * p + 1], 4)
-        sent(4 * p + 3, sback.at[p], rback.at[p], 4)
-    green_sent()
-    for copy in halo_copies + rim_copies:
+    pass_sent(1)
+    for copy in rim_copies:
         copy.wait_send()
 
 

time: 78.7 us -> 78.1 us (level)
  no operation moved by 1% of the time
where the time goes in v8:
time: 78.1 us; the launch traced here: 77.9 us
  Pallas kernels  75.8 us (97%)
  local copies, waits for them, and re-layouts  1.4 us (2%)
    pallas_call x1, Pallas kernels, local(): pl.pallas_call(kernel, out_shape=jax.ShapeDtypeStruct((128, LANES), F32),...  75.8 us

profile of v8, /device:TPU:1, one launch (start us, length us, event | category | flops | bytes accessed | tf_op | source)
XLA Modules:
  0.0 77.9 jit_solution(5596803630386342835)
XLA Ops:
  0.6 75.8 %panel_solver.1 = f32[128,128]{1,0:T(8,128)} custom-call(bf16[64,128]{1,0:T(8,128)(2,1)} %bitcast.14, f32[64,128]{1,0:T(8,128)} %bitcast.13, bf16[8192,256]{1,0:T(8,128)(2,1)} %bitcast.11, bf16[128,4,4096]{2,1,0:T(4,128)(2,1)} %near_hbm.1, f32[32,4096]{1,0:T(8,128)} %bitcast.12, s32[1,128]{1,0:T(1,128)} %bitcast.16, s32[1,128]{1,0:T(1,128)} %bitcast.17, ...), custom_call_target="tpu_custom_call" | custom-call | tf_op jit(solution)/shard_map/panel_solver/pallas_call | solution.py:787
  76.5 1.4 %slice_bitcast_fusion = (f32[8192]{0:T(1024)}, f32[8192]{0:T(1024)}) fusion(f32[128,128]{1,0:T(8,128)} %panel_solver.1), kind=kLoop, calls=%fused_computation | loop fusion | bytes 131072 | tf_op jit(solution)/shard_map/reshape | solution.py:842

commit v9 on v8

--- a/solution.py
+++ b/solution.py
@@ -648,6 +648,7 @@
         @pl.when(last)
         def _():
             exchange(4, swords.at[5], rwords.at[5], 4, 2)
+            fold(0, near[...])
             near_adjoint()
             arrived(4, swords.at[5], rwords.at[5], 2)
 
@@ -757,7 +758,7 @@
         def _():
             pot = far + near[...]
             val[...] = (pot - goal[...]).astype(BF16).astype(F32)
-            fold(0, pot)
+            near[...] = pot
 
         @pl.when(last)
         def _():

time: 78.1 us -> 78.1 us (level)
  no operation moved by 1% of the time
where the time goes in v9:
time: 78.1 us; the launch traced here: 77.9 us
  Pallas kernels  75.8 us (97%)
  local copies, waits for them, and re-layouts  1.4 us (2%)
    pallas_call x1, Pallas kernels, local(): pl.pallas_call(kernel, out_shape=jax.ShapeDtypeStruct((128, LANES), F32),...  75.8 us

profile of v9, /device:TPU:1, one launch (start us, length us, event | category | flops | bytes accessed | tf_op | source)
XLA Modules:
  0.0 77.9 jit_solution(7153300183550725789)
XLA Ops:
  0.6 75.8 %panel_solver.1 = f32[128,128]{1,0:T(8,128)} custom-call(bf16[64,128]{1,0:T(8,128)(2,1)} %bitcast.14, f32[64,128]{1,0:T(8,128)} %bitcast.13, bf16[8192,256]{1,0:T(8,128)(2,1)} %bitcast.11, bf16[128,4,4096]{2,1,0:T(4,128)(2,1)} %near_hbm.1, f32[32,4096]{1,0:T(8,128)} %bitcast.12, s32[1,128]{1,0:T(1,128)} %bitcast.16, s32[1,128]{1,0:T(1,128)} %bitcast.17, ...), custom_call_target="tpu_custom_call" | custom-call | tf_op jit(solution)/shard_map/panel_solver/pallas_call | solution.py:788
  76.5 1.4 %slice_bitcast_fusion = (f32[8192]{0:T(1024)}, f32[8192]{0:T(1024)}) fusion(f32[128,128]{1,0:T(8,128)} %panel_solver.1), kind=kLoop, calls=%fused_computation | loop fusion | bytes 131072 | tf_op jit(solution)/shard_map/reshape | solution.py:843
